TPU v7x, 32 devices: a whole 2x2x4 slice. The times are simulated.
32 devices in a mesh: expert: 4 (over y, core), row: 8 (over z, x).
Axes of the slice: x: 2, y: 2, z: 4, core: 2. Of those that a mesh axis runs over, the one named last changes fastest.
Arguments:
- sampled: int32 [4, 32], P('expert'), may hold values from 0 to 31, each once within a row
- refresh: int32 [64], P('expert'), may hold values 0 or 1
- momentum_bank: bfloat16 [128, 2048, 512], P('expert', 'row'), may hold values from -6 to 6
- weights: bfloat16 [64, 2048, 512], P('expert', 'row'), may hold values from -6 to 6
- grads: bfloat16 [64, 2048, 512], P('expert', 'row'), may hold values from -6 to 6
- basis: float32 [64, 2048, 64], P('expert', 'row'), may hold values from -0.125 to 0.125
Outputs:
- new_bank: bfloat16 [128, 2048, 512], P('expert', 'row')
- new_weights: bfloat16 [64, 2048, 512], P('expert', 'row')
Inputs may be any that keep to these rules, and one draw needn't show every extreme that they name: Each row of sampled names every number of 0 to 31 once.
All inputs are finite; a program needn't handle non-finite values. No bound on the sum of `refresh` on one device may be relied on, other than what follows from the above.
Results may differ from a plain program's by a relative error of at most 0.0045.
Values may be sent and summed in bfloat16 or wider, within the bound.
A program may use at most 128 MiB of HBM per device.

v0:
```python
import math

import jax
import jax.numpy as jnp
from jax import lax
from jax.sharding import PartitionSpec as P

D = 2048
FF = 512
ITERS = 3


momentum_decay = 0.9
residual_weight = 2.0
step_rate = 0.5
decay_rate = 0.1
coef_first = 3.4445
coef_second = -4.775
coef_third = 2.0315
epsilon = 1e-07


def orthogonalize(block):
    matrices = block[0]
    values = matrices.astype(jnp.float32)
    total_norm = jnp.sqrt(jnp.sum(values * values, axis=(1, 2), keepdims=True)) + epsilon
    iterate = (values / total_norm).astype(jnp.bfloat16)
    for sweep in range(ITERS):
        gram = jnp.einsum(
            "mdi,mdj->mij", iterate, iterate, preferred_element_type=jnp.float32
        ).astype(jnp.bfloat16)
        square = jnp.einsum("mij,mjk->mik", gram, gram, preferred_element_type=jnp.float32)
        gram_full = lax.optimization_barrier(gram).astype(jnp.float32)
        poly = (coef_second * gram_full + coef_third * square).astype(jnp.bfloat16)
        product = jnp.einsum("mdi,mij->mdj", iterate, poly, preferred_element_type=jnp.float32)
        iterate = (coef_first * iterate.astype(jnp.float32) + product).astype(jnp.bfloat16)
    return iterate[None]


def shards(sampled, refresh, momentum_bank, weights, grads, basis):
    group_count = weights.shape[0]
    chosen = sampled[0, :group_count]
    old = momentum_bank[chosen].astype(jnp.float32)
    basis_high = basis.astype(jnp.bfloat16)
    basis_low = (basis - basis_high.astype(jnp.float32)).astype(jnp.bfloat16)
    partial_sum = jnp.einsum("srk,srf->skf", basis_high, grads, preferred_element_type=jnp.float32)
    partial_sum = partial_sum + jnp.einsum(
        "srk,srf->skf", basis_low, grads, preferred_element_type=jnp.float32
    )
    proj = lax.psum(partial_sum.astype(jnp.bfloat16), "row").astype(jnp.float32)
    low = jnp.einsum("srk,skf->srf", basis, proj, precision=lax.Precision.HIGH)
    weight_flag = refresh.astype(jnp.float32)[:, None, None]
    grad_full = grads.astype(jnp.float32)
    mom = (momentum_decay * old + low + residual_weight * weight_flag * (grad_full - low)).astype(
        jnp.bfloat16
    )
    new_bank = momentum_bank.at[chosen].set(mom)
    owners = lax.axis_size("row")
    row_count = weights.shape[1]
    per_owner = weights.shape[0] // owners
    packed = mom.reshape(owners, per_owner, row_count, weights.shape[2])
    gathered = lax.all_to_all(packed, "row", split_axis=0, concat_axis=2, tiled=True)
    result = orthogonalize(gathered)
    returned = lax.all_to_all(result, "row", split_axis=2, concat_axis=0, tiled=True)
    ortho = returned.reshape(weights.shape)
    scale_step = step_rate * 0.2 * math.sqrt(max(D, FF))
    updated = weights.astype(jnp.float32) * (
        1.0 - step_rate * decay_rate
    ) - scale_step * ortho.astype(jnp.float32)
    return (new_bank, updated.astype(jnp.bfloat16))


def solution(mesh):
    in_specs = (
        P("expert", None),
        P("expert"),
        P("expert", "row", None),
        P("expert", "row", None),
        P("expert", "row", None),
        P("expert", "row", None),
    )
    out_specs = (P("expert", "row", None), P("expert", "row", None))
    return jax.shard_map(shards, mesh=mesh, in_specs=in_specs, out_specs=out_specs, check_vma=False)
```

profile of v0, /device:TPU:24, one launch (start us, length us, event | category | flops | bytes accessed | tf_op | source)
XLA Modules:
  0.0 388.9 jit_solution(5933377888364387182)
XLA Ops:
  7.2 0.0 copy-start.5
  7.2 0.0 all-reduce.2.cloned.1.call-start
  7.2 0.0 copy-start
  7.2 7.8 %copy.38 = bf16[32,256,512]{2,1,0:T(8,128)(2,1)} copy(bf16[32,256,512]{2,1,0:T(8,128)(2,1)} %param.8) | data formatting | bytes 16777216
  15.0 0.0 copy-done.5
  15.0 0.0 copy-done
  15.0 0.8 fusion.7
  15.9 1.8 add_convert_fusion.6
  17.7 0.0 all-reduce.2.cloned.1.call-update
  17.7 0.0 copy-start.6
  17.7 6.4 %copy.24 = bf16[16,256,512]{1,2,0:T(8,128)(2,1)} copy(bf16[16,256,512]{2,1,0:T(8,128)(2,1)} %param.10) | data formatting | bytes 8388608 | tf_op args[4]
  24.1 0.0 copy-done.6
  24.1 6.2 %gather_fusion = bf16[16,256,512]{2,1,0:T(8,128)(2,1)} fusion(bf16[32,256,512]{2,1,0:T(8,128)(2,1)} %copy.38, s32[1024]{0:T(1024)S(1)} %pad_clamp_fusion), kind=kCustom, calls=%fused_computation | custom fusion | bytes 8388672 | tf_op jit(solution)/shard_map/gather | solution.py:43
  30.4 0.0 copy-start.7
  30.4 6.4 %copy.23 = bf16[16,256,512]{1,2,0:T(8,128)(2,1)} copy(bf16[16,256,512]{2,1,0:T(8,128)(2,1)} %gather_fusion) | data formatting | bytes 8388608 | tf_op jit(solution)/shard_map/gather | solution.py:43
  36.8 0.0 copy-done.7
  36.8 59.2 %all-reduce.2.cloned.1.call-done = bf16[16,64,512]{2,1,0:T(8,128)(2,1)} async-done(((bf16[16,64,512]{2,1,0:T(8,128)(2,1)}), bf16[16,64,512]{2,1,0:T(8,128)(2,1)}) %all-reduce.2.cloned.1.call-update) | async-done | bytes 1048592 | tf_op jit(solution)/shard_map/psum | solution.py:50
  96.0 8.0 %fusion.3 = bf16[16,256,512]{1,2,0:T(8,128)(2,1)S(1)} fusion(bf16[16,256,512]{1,2,0:T(8,128)(2,1)} %copy.24, bf16[16,256,512]{1,2,0:T(8,128)(2,1)} %copy.23, f32[16]{0:T(128)S(1)} %convert_multiply_fusion.2, bf16[16,64,512]{2,1,0:T(8,128)(2,1)} %all-reduce.2.cloned.1.call-done, f32[16,256,64]{1,2,0:T(8,128)S(1)} %copy-done.5), kind=kOutput, calls=%fused_computation.10 | convolution fusion | flops 822083584 | bytes 14680128 | tf_op jit(solution)/shard_map/srk,skf->srf/dot_general | solution.py:51
  104.0 0.0 copy-start.2
  104.0 95.5 %all_to_all.8 = bf16[8,2,256,512]{2,3,1,0:T(8,128)(2,1)S(1)} all-to-all(bf16[8,2,256,512]{2,3,1,0:T(8,128)(2,1)S(1)} %bitcast.51), channel_id=1, replica_groups=mesh['expert'=4,'row'=8] {'row'}, dimensions={0} | all-to-all | bytes 8388608 | tf_op jit(solution)/shard_map/all_to_all | solution.py:62
  199.6 0.0 copy-done.2
  199.6 0.0 copy-start.1
  199.6 1.9 copy-done.1
  201.5 4.1 %convert_bitcast_fusion = f32[1,2,8,256,512]{3,4,1,2,0:T(8,128)} fusion(bf16[8,2,256,512]{2,3,1,0:T(8,128)(2,1)S(1)} %all_to_all.8), kind=kLoop, calls=%fused_computation.3 | loop fusion | flops 2097152 | bytes 12582912 | tf_op jit(solution)/shard_map/convert_element_type | solution.py:25
  205.6 8.7 %copy.26 = f32[1,2,8,256,512]{4,3,2,1,0:T(8,128)} copy(f32[1,2,8,256,512]{3,4,1,2,0:T(8,128)} %convert_bitcast_fusion) | data formatting | bytes 16777216 | tf_op jit(solution)/shard_map/convert_element_type | solution.py:25
  214.3 3.4 fusion
  217.7 4.6 %divide_convert_fusion = bf16[2,2048,512]{2,1,0:T(8,128)(2,1)S(1)} fusion(f32[2,2048,512]{2,1,0:T(8,128)} %bitcast.49, f32[2]{0:T(128)S(1)} %sqrt_add_fusion), kind=kLoop, calls=%fused_computation.16 | loop fusion | flops 4194304 | bytes 12582920 | tf_op jit(solution)/shard_map/convert_element_type | solution.py:27
  222.3 0.0 copy-start.3
  222.3 2.0 copy-done.3
  224.3 2.4 convolution_convert_fusion.2
  226.7 7.6 %add_convert_fusion.2 = bf16[2,2048,512]{2,1,0:T(8,128)(2,1)} fusion(bf16[2,2048,512]{2,1,0:T(8,128)(2,1)} %copy-done.3, bf16[2,512,512]{2,1,0:T(8,128)(2,1)S(1)} %convolution_convert_fusion.2), kind=kOutput, calls=%fused_computation.15 | convolution fusion | flops 2695364608 | bytes 9437184 | tf_op jit(solution)/shard_map/mdi,mij->mdj/dot_general | solution.py:35
  234.3 5.8 %convolution_convert_fusion.1 = bf16[2,512,512]{2,1,0:T(8,128)(2,1)S(1)} fusion(bf16[2,2048,512]{2,1,0:T(8,128)(2,1)} %add_convert_fusion.2), kind=kOutput, calls=%fused_computation.23 | convolution fusion | flops 2148007936 | bytes 5242880 | tf_op jit(solution)/shard_map/mdi,mdj->mij/dot_general | solution.py:29
  240.1 7.6 %add_convert_fusion.1 = bf16[2,2048,512]{2,1,0:T(8,128)(2,1)} fusion(bf16[2,2048,512]{2,1,0:T(8,128)(2,1)} %add_convert_fusion.2, bf16[2,512,512]{2,1,0:T(8,128)(2,1)S(1)} %convolution_convert_fusion.1), kind=kOutput, calls=%fused_computation.14 | convolution fusion | flops 2695364608 | bytes 9437184 | tf_op jit(solution)/shard_map/mdi,mij->mdj/dot_general | solution.py:35
  247.7 5.8 %convolution_convert_fusion = bf16[2,512,512]{2,1,0:T(8,128)(2,1)S(1)} fusion(bf16[2,2048,512]{2,1,0:T(8,128)(2,1)} %add_convert_fusion.1), kind=kOutput, calls=%fused_computation.22 | convolution fusion | flops 2148007936 | bytes 5242880 | tf_op jit(solution)/shard_map/mdi,mdj->mij/dot_general | solution.py:29
  253.5 7.5 %fusion.5 = bf16[1,2,2048,512]{3,2,1,0:T(8,128)(2,1)} fusion(bf16[2,2048,512]{2,1,0:T(8,128)(2,1)} %add_convert_fusion.1, bf16[2,512,512]{2,1,0:T(8,128)(2,1)S(1)} %convolution_convert_fusion), kind=kOutput, calls=%fused_computation.17 | convolution fusion | flops 2695364608 | bytes 9437184 | tf_op jit(solution)/shard_map/mdi,mij->mdj/dot_general | solution.py:35
  261.1 10.1 %copy.30 = bf16[1,2,2048,512]{3,1,0,2:T(2,128)(2,1)} copy(bf16[1,2,2048,512]{3,2,1,0:T(8,128)(2,1)} %fusion.5) | data formatting | bytes 8388608 | tf_op jit(solution)/shard_map/broadcast_in_dim | solution.py:37
  271.2 7.4 %all-to-all-start.1 = ((bf16[1,2,2048,512]{3,1,0,2:T(2,128)(2,1)}), bf16[1,2,2048,512]{3,1,0,2:T(2,128)(2,1)}, u32[]{:S(2)}, u32[]{:S(2)}) async-start(bf16[1,2,2048,512]{3,1,0,2:T(2,128)(2,1)} %copy.30), calls=%async_computation.1 | async-start | bytes 8388608 | tf_op jit(solution)/shard_map/all_to_all | solution.py:64
  278.6 6.4 %copy.25 = bf16[16,256,512]{2,1,0:T(8,128)(2,1)} copy(bf16[16,256,512]{1,2,0:T(8,128)(2,1)} %copy-done.2) | data formatting | bytes 8388608 | tf_op jit(solution)/shard_map/convert_element_type | solution.py:54
  284.9 10.8 %scatter_fusion = bf16[32,256,512]{2,1,0:T(8,128)(2,1)} fusion(bf16[32,256,512]{2,1,0:T(8,128)(2,1)} %copy.38, s32[16]{0:T(128)S(1)} %fusion.9, bf16[16,256,512]{2,1,0:T(8,128)(2,1)} %copy.25), kind=kCustom, calls=%fused_computation.1 | custom fusion | bytes 12582976 | tf_op jit(solution)/shard_map/scatter | solution.py:57
  295.8 73.5 %all-to-all-done.1 = bf16[1,2,2048,512]{3,1,0,2:T(2,128)(2,1)} async-done(((bf16[1,2,2048,512]{3,1,0,2:T(2,128)(2,1)}), bf16[1,2,2048,512]{3,1,0,2:T(2,128)(2,1)}, u32[]{:S(2)}, u32[]{:S(2)}) %all-to-all-start.1) | async-done | bytes 4194336 | tf_op jit(solution)/shard_map/all_to_all | solution.py:64
  369.3 5.5 %convert_multiply_fusion.1 = f32[1,2,2048,512]{3,1,0,2:T(2,128)S(1)} fusion(bf16[1,2,2048,512]{3,1,0,2:T(2,128)(2,1)} %all-to-all-done.1), kind=kLoop, calls=%fused_computation.12 | loop fusion | flops 4194304 | bytes 12582912 | tf_op jit(solution)/shard_map/mul | solution.py:69
  374.8 0.0 copy-start.4
  374.8 1.6 copy.31
  376.4 0.6 copy-done.4
  377.0 5.0 %fusion.1 = bf16[16,256,512]{2,1,0:T(8,128)(2,1)} fusion(f32[8,1,2,256,512]{4,3,2,0,1:T(8,128)S(1)} %copy.31, bf16[16,256,512]{2,1,0:T(8,128)(2,1)S(1)} %copy-done.4), kind=kLoop, calls=%fused_computation.6 | loop fusion | flops 8388608 | bytes 16777216 | tf_op jit(solution)/shard_map/convert_element_type | solution.py:70
  (4 shorter events, 0.0 us)
Async XLA Ops:
  7.2 7.9 %copy-start.5 = (f32[16,256,64]{1,2,0:T(8,128)S(1)}, f32[16,256,64]{1,2,0:T(8,128)}, u32[]{:S(2)}) copy-start(f32[16,256,64]{1,2,0:T(8,128)} %param.11) | copy-start | bytes 3145732
  7.2 88.8 %all-reduce.2.cloned.1.call-start = ((), (), s32[]{:S(2)}) async-start(), calls=%async_computation.2 | async-start | bytes 2097152 | tf_op jit(solution)/shard_map/psum | solution.py:50
  7.2 7.8 %copy-start = (bf16[16,256,512]{2,1,0:T(8,128)(2,1)S(1)}, bf16[16,256,512]{2,1,0:T(8,128)(2,1)}, u32[]{:S(2)}) copy-start(bf16[16,256,512]{2,1,0:T(8,128)(2,1)} %param.10) | copy-start | bytes 12582916
  17.7 6.4 %copy-start.6 = (s32[1,32]{1,0:T(1,128)S(1)}, s32[1,32]{1,0:T(1,128)}, u32[]{:S(2)}) copy-start(s32[1,32]{1,0:T(1,128)} %param.6) | copy-start | bytes 388
  30.4 6.4 %copy-start.7 = (s32[16]{0:T(128)S(1)}, s32[16]{0:T(128)}, u32[]{:S(2)}) copy-start(s32[16]{0:T(128)} %param.7) | copy-start | bytes 196
  104.0 95.5 %copy-start.2 = (bf16[16,256,512]{1,2,0:T(8,128)(2,1)}, bf16[16,256,512]{1,2,0:T(8,128)(2,1)S(1)}, u32[]{:S(2)}) copy-start(bf16[16,256,512]{1,2,0:T(8,128)(2,1)S(1)} %fusion.3) | copy-start | bytes 12582916
  199.6 1.9 copy-start.1
  222.3 2.0 copy-start.3
  271.2 98.1 %all-to-all-start.1 = ((bf16[1,2,2048,512]{3,1,0,2:T(2,128)(2,1)}), bf16[1,2,2048,512]{3,1,0,2:T(2,128)(2,1)}, u32[]{:S(2)}, u32[]{:S(2)}) async-start(bf16[1,2,2048,512]{3,1,0,2:T(2,128)(2,1)} %copy.30), calls=%async_computation.1 | async-start | bytes 8388608 | tf_op jit(solution)/shard_map/all_to_all | solution.py:64
  374.8 2.2 copy-start.4
Sparse Core Ops, SparseCore 0:
  17.8 78.0 all-reduce.1
where the time goes:
time: 393 us; the launch traced here: 389 us
  waiting for transfers between devices  133 us (34%)
  blocking collectives  95.5 us (24%)
  local copies, waits for them, and re-layouts  69 us (18%)
  matrix products  47.4 us (12%)
  other arithmetic  22.7 us (6%)
  between operations  14.1 us (4%)
  starting transfers between devices  7.42 us (2%)
    all_to_all x1, blocking collectives, shards(): lax.all_to_all(packed, 'row', split_axis=0, concat_axis=2, tiled=True)  95.5 us
    all_to_all x1, waiting for transfers between devices, shards(): lax.all_to_all(result, 'row', split_axis=2, concat_axis=0, tiled=True)  73.5 us
    psum x1, waiting for transfers between devices, shards(): proj = lax.psum(partial_sum.astype(jnp.bfloat16), 'row').astype(jnp.float32)  59.2 us
    dot_general x3, matrix products, orthogonalize(): jnp.einsum('mdi,mij->mdj', iterate, poly, preferred_element_type=jnp.floa...  22.7 us
    unnamed x18, local copies, waits for them, and re-layouts  18.7 us
    dot_general x3, matrix products, orthogonalize(): jnp.einsum('mdi,mdj->mij', iterate, iterate, preferred_element_type=jnp.f...  14 us
    gather x2, local copies, waits for them, and re-layouts, shards(): old = momentum_bank[chosen].astype(jnp.float32)  12.7 us
    scatter x1, local copies, waits for them, and re-layouts, shards(): new_bank = momentum_bank.at[chosen].set(mom)  10.8 us
  transfers between devices with their start and end apart: 2, of which 2 were waited for; matrix products, arithmetic and copies ran while one was open for 9% of the time, Pallas kernels for 0%

commit v1 on v0

v1 whole, which is shorter than its diff:
```python
import math

import jax
import jax.numpy as jnp
from jax import lax
from jax.sharding import PartitionSpec as P

D = 2048
FF = 512
ITERS = 3


momentum_decay = 0.9
residual_weight = 2.0
step_rate = 0.5
decay_rate = 0.1
coef_first = 3.4445
coef_second = -4.775
coef_third = 2.0315
epsilon = 1e-07
TILE = 128


def pack_upper(full):
    width = full.shape[-1]
    return jnp.concatenate(
        [full[:, at : at + TILE, at:] for at in range(0, width, TILE)], axis=2
    )


def unpack_upper(packed, width):
    rows = []
    offset = 0
    tiles = {}
    count = width // TILE
    for i in range(count):
        for j in range(i, count):
            tile = packed[:, :, offset : offset + TILE]
            tiles[i, j] = tile
            if j > i:
                tiles[j, i] = jnp.swapaxes(tile, 1, 2)
            offset += TILE
    for i in range(count):
        rows.append(jnp.concatenate([tiles[i, j] for j in range(count)], axis=2))
    return jnp.concatenate(rows, axis=1)


def mm(a, b):
    return jnp.einsum(
        "mij,mjk->mik",
        a.astype(jnp.bfloat16),
        b.astype(jnp.bfloat16),
        preferred_element_type=jnp.float32,
    )


def factors(gram):
    width = gram.shape[-1]
    eye = jnp.eye(width, dtype=jnp.float32)
    total = jnp.sum(gram * eye, axis=(1, 2), keepdims=True)
    inverse = 1.0 / (jnp.sqrt(total) + epsilon)
    a = gram * inverse * inverse
    q = None
    for sweep in range(ITERS):
        poly = coef_second * a + coef_third * mm(a, a)
        q = coef_first * eye + poly if q is None else coef_first * q + mm(q, poly)
        if sweep < ITERS - 1:
            half = coef_first * a + mm(a, poly)
            a = coef_first * half + mm(poly, half)
    return q * inverse


def shards(sampled, refresh, momentum_bank, weights, grads, basis):
    group_count = weights.shape[0]
    width = weights.shape[2]
    chosen = sampled[0, :group_count]
    old = momentum_bank[chosen].astype(jnp.float32)
    basis_high = basis.astype(jnp.bfloat16)
    partial_sum = jnp.einsum("srk,srf->skf", basis_high, grads, preferred_element_type=jnp.float32)
    proj = lax.psum(partial_sum.astype(jnp.bfloat16), "row")
    low = jnp.einsum("srk,skf->srf", basis_high, proj, preferred_element_type=jnp.float32)
    weight_flag = refresh.astype(jnp.float32)[:, None, None]
    grad_full = grads.astype(jnp.float32)
    mom = (momentum_decay * old + low + residual_weight * weight_flag * (grad_full - low)).astype(
        jnp.bfloat16
    )
    new_bank = momentum_bank.at[chosen].set(mom)
    partial_gram = jnp.einsum("srf,srg->sfg", mom, mom, preferred_element_type=jnp.float32)
    packed = pack_upper(partial_gram).astype(jnp.bfloat16)
    summed = lax.psum_scatter(packed, "row", scatter_dimension=0, tiled=True)
    q = factors(unpack_upper(summed.astype(jnp.float32), width))
    sent = pack_upper(q.astype(jnp.bfloat16))
    everyone = lax.all_gather(sent, "row", axis=0, tiled=True)
    q_full = unpack_upper(everyone, width)
    ortho = jnp.einsum("srf,sfg->srg", mom, q_full, preferred_element_type=jnp.float32)
    scale_step = step_rate * 0.2 * math.sqrt(max(D, FF))
    updated = weights.astype(jnp.float32) * (1.0 - step_rate * decay_rate) - scale_step * ortho
    return (new_bank, updated.astype(jnp.bfloat16))


def solution(mesh):
    in_specs = (
        P("expert", None),
        P("expert"),
        P("expert", "row", None),
        P("expert", "row", None),
        P("expert", "row", None),
        P("expert", "row", None),
    )
    out_specs = (P("expert", "row", None), P("expert", "row", None))
    return jax.shard_map(shards, mesh=mesh, in_specs=in_specs, out_specs=out_specs, check_vma=False)
```

time: 393 us -> 365 us (0.929)
  waiting for transfers between devices: 133 us -> 229 us
  blocking collectives: 95.5 us -> 0 us
  other arithmetic: 22.7 us -> 6.96 us
  matrix products: 47.4 us -> 36 us
  starting transfers between devices: 7.42 us -> 0.3 us
  local copies, waits for them, and re-layouts: 69 us -> 74.6 us
    reduce_scatter x0 -> x1, waiting for transfers between devices: none -> 102 us  [shards(): summed = lax.psum_scatter(packed, 'row', scatter_dimension=0, tiled=True)]
    all_to_all x1 -> x0, blocking collectives: 95.5 us -> none  [shards(): lax.all_to_all(packed, 'row', split_axis=0, concat_axis=2, tiled=True)]
    all_to_all x1 -> x0, waiting for transfers between devices: 73.5 us -> none  [shards(): lax.all_to_all(result, 'row', split_axis=2, concat_axis=0, tiled=True)]
    all_gather x0 -> x1, waiting for transfers between devices: none -> 67.6 us  [shards(): everyone = lax.all_gather(sent, 'row', axis=0, tiled=True)]
    slice x0 -> x17, local copies, waits for them, and re-layouts: none -> 15.2 us  [the longest x9 9.41 us: unpack_upper(): tile = packed[:, :, offset:offset + TILE]]
    convert_element_type x3 -> x1, other arithmetic: 13.8 us -> 0.11 us  [factors(): eye = jnp.eye(width, dtype=jnp.float32)]
    dot_general x8 -> x11, matrix products: 46.6 us -> 34.2 us  [the longest x8 14.3 us: mm(): jnp.einsum('mij,mjk->mik', a.astype(jnp.bfloat16), b.astype(jnp.bfloat16)...]
    broadcast_in_dim x1 -> x0, local copies, waits for them, and re-layouts: 10.1 us -> none  [orthogonalize(): return iterate[None]]
  transfers between devices with their start and end apart: 2 -> 3, of which waited for: 2 -> 3; matrix products, arithmetic and copies ran while one was open for 9% -> 10% of each run, Pallas kernels for 0% -> 0%
where the time goes in v1:
time: 365 us; the launch traced here: 361 us
  waiting for transfers between devices  229 us (63%)
  local copies, waits for them, and re-layouts  74.6 us (20%)
  matrix products  36 us (10%)
  between operations  14 us (4%)
  other arithmetic  6.96 us (2%)
    reduce_scatter x1, waiting for transfers between devices, shards(): summed = lax.psum_scatter(packed, 'row', scatter_dimension=0, tiled=True)  102 us
    all_gather x1, waiting for transfers between devices, shards(): everyone = lax.all_gather(sent, 'row', axis=0, tiled=True)  67.6 us
    psum x1, waiting for transfers between devices, shards(): proj = lax.psum(partial_sum.astype(jnp.bfloat16), 'row')  59.1 us
    unnamed x44, local copies, waits for them, and re-layouts  28.1 us
    dot_general x8, matrix products, mm(): jnp.einsum('mij,mjk->mik', a.astype(jnp.bfloat16), b.astype(jnp.bfloat16)...  14.3 us
    gather x2, local copies, waits for them, and re-layouts, shards(): old = momentum_bank[chosen].astype(jnp.float32)  12.7 us
    scatter x1, local copies, waits for them, and re-layouts, shards(): new_bank = momentum_bank.at[chosen].set(mom)  11 us
    slice x9, local copies, waits for them, and re-layouts, unpack_upper(): tile = packed[:, :, offset:offset + TILE]  9.41 us
  transfers between devices with their start and end apart: 3, of which 3 were waited for; matrix products, arithmetic and copies ran while one was open for 10% of the time, Pallas kernels for 0%

profile of v1, /device:TPU:24, one launch (start us, length us, event | category | flops | bytes accessed | tf_op | source)
XLA Modules:
  0.0 360.8 jit_solution(13147133765897437609)
XLA Ops:
  7.2 7.8 %copy.156 = bf16[32,256,512]{2,1,0:T(8,128)(2,1)} copy(bf16[32,256,512]{2,1,0:T(8,128)(2,1)} %param.8) | data formatting | bytes 16777216
  15.0 1.8 convolution_convert_fusion.1
  17.0 6.4 %copy.80 = bf16[16,256,512]{1,2,0:T(8,128)(2,1)} copy(bf16[16,256,512]{2,1,0:T(8,128)(2,1)} %param.10) | data formatting | bytes 8388608 | tf_op args[4]
  23.4 6.2 %gather_fusion = bf16[16,256,512]{2,1,0:T(8,128)(2,1)} fusion(bf16[32,256,512]{2,1,0:T(8,128)(2,1)} %copy.156, s32[1024]{0:T(1024)S(1)} %pad_clamp_fusion), kind=kCustom, calls=%fused_computation | custom fusion | bytes 8388672 | tf_op jit(solution)/shard_map/gather | solution.py:77
  29.6 6.4 %copy.79 = bf16[16,256,512]{1,2,0:T(8,128)(2,1)} copy(bf16[16,256,512]{2,1,0:T(8,128)(2,1)} %gather_fusion) | data formatting | bytes 8388608 | tf_op jit(solution)/shard_map/gather | solution.py:77
  36.1 59.1 %all-reduce.2.cloned.1.call-done = bf16[16,64,512]{2,1,0:T(8,128)(2,1)} async-done(((bf16[16,64,512]{2,1,0:T(8,128)(2,1)}), bf16[16,64,512]{2,1,0:T(8,128)(2,1)}) %all-reduce.2.cloned.1.call-update) | async-done | bytes 1048592 | tf_op jit(solution)/shard_map/psum | solution.py:80
  95.2 6.5 %fusion.21 = bf16[16,256,512]{1,2,0:T(8,128)(2,1)S(1)} fusion(bf16[16,256,512]{1,2,0:T(8,128)(2,1)} %copy.80, bf16[16,256,512]{1,2,0:T(8,128)(2,1)} %copy.79, f32[16]{0:T(128)S(1)} %convert_multiply_fusion, bf16[16,64,512]{2,1,0:T(8,128)(2,1)} %all-reduce.2.cloned.1.call-done, f32[16,256,64]{1,2,0:T(8,128)S(1)} %copy-done.5), kind=kOutput, calls=%fused_computation.25 | convolution fusion | flops 285474816 | bytes 14680128 | tf_op jit(solution)/shard_map/srk,skf->srf/dot_general | solution.py:81
  101.6 5.6 %convolution_convert_fusion = bf16[16,512,512]{1,2,0:T(8,128)(2,1)} fusion(bf16[16,256,512]{1,2,0:T(8,128)(2,1)S(1)} %fusion.21), kind=kOutput, calls=%fused_computation.28 | convolution fusion | flops 2151677952 | bytes 12582912 | tf_op jit(solution)/shard_map/srf,srg->sfg/dot_general | solution.py:88
  107.2 1.7 slice.128
  109.0 1.6 slice.129
  110.5 1.3 slice.130
  111.9 1.1 slice.131
  113.0 6.2 %pad_maximum_fusion = bf16[16,128,1280]{1,2,0:T(8,128)(2,1)} fusion(bf16[16,128,128]{1,2,0:T(8,128)(2,1)S(1)} %slice.131, bf16[16,128,256]{1,2,0:T(8,128)(2,1)S(1)} %slice.130, bf16[16,128,384]{1,2,0:T(8,128)(2,1)S(1)} %slice.129, bf16[16,128,512]{1,2,0:T(8,128)(2,1)S(1)} %slice.128), kind=kLoop, calls=%fused_computation.29 | loop fusion | flops 20971520 | bytes 10485760 | tf_op jit(solution)/shard_map/concatenate | solution.py:26
  119.3 0.2 all-gather.2.cloned.1.call-start
  119.7 102.2 %reduce-scatter.2.cloned.1.call-done = bf16[2,128,1280]{1,2,0:T(8,128)(2,1)} async-done(((bf16[16,128,1280]{1,2,0:T(8,128)(2,1)}), bf16[2,128,1280]{1,2,0:T(8,128)(2,1)}) %reduce-scatter.2.cloned.1.call-update) | async-done | bytes 655376 | tf_op jit(solution)/shard_map/reduce_scatter | solution.py:90
  221.9 1.8 fusion.51
  223.8 0.7 copy.141
  224.5 0.8 copy.142
  225.3 0.8 copy.143
  226.0 0.7 copy.144
  226.8 0.8 copy.145
  227.5 0.7 copy.146
  228.4 0.7 copy-done.11
  229.2 0.4 multiply_reduce_fusion
  229.7 1.2 multiply_add_fusion.5
  230.9 1.1 multiply_add_fusion.3
  232.0 0.7 multiply_add_fusion.2
  232.7 0.8 add_convert_fusion.1
  233.5 0.7 multiply_add_fusion.1
  234.2 2.1 multiply_add_fusion
  236.3 2.2 multiply_add_fusion.4
  238.4 5.5 %multiply_convert_fusion = bf16[2,512,512]{1,2,0:T(8,128)(2,1)S(1)} fusion(f32[2,512,512]{1,2,0:T(8,128)} %multiply_add_fusion.4, f32[2,512,512]{1,2,0:T(8,128)} %multiply_add_fusion, f32[2]{0:T(128)S(1)} %add_divide_fusion), kind=kOutput, calls=%fused_computation.31 | convolution fusion | flops 1078984704 | bytes 5242888 | tf_op jit(solution)/shard_map/mij,mjk->mik/dot_general | solution.py:49
  244.2 1.1 copy.110
  245.3 6.5 %copy.81 = bf16[16,256,512]{2,1,0:T(8,128)(2,1)} copy(bf16[16,256,512]{1,2,0:T(8,128)(2,1)} %copy-done) | data formatting | bytes 8388608 | tf_op jit(solution)/shard_map/convert_element_type | solution.py:84
  251.7 11.0 %scatter_fusion = bf16[32,256,512]{2,1,0:T(8,128)(2,1)} fusion(bf16[32,256,512]{2,1,0:T(8,128)(2,1)} %copy.156, s32[16]{0:T(128)S(1)} %fusion.46, bf16[16,256,512]{2,1,0:T(8,128)(2,1)} %copy.81), kind=kCustom, calls=%fused_computation.1 | custom fusion | bytes 12582976 | tf_op jit(solution)/shard_map/scatter | solution.py:87
  262.8 67.6 %all-gather.2.cloned.1.call-done = bf16[16,128,1280]{2,1,0:T(8,128)(2,1)} async-done(((bf16[2,128,1280]{2,1,0:T(8,128)(2,1)}), bf16[16,128,1280]{2,1,0:T(8,128)(2,1)}) %all-gather.2.cloned.1.call-update) | async-done | bytes 5242896 | tf_op jit(solution)/shard_map/all_gather | solution.py:93
  330.4 3.5 fusion.50
  333.9 1.0 copy.148
  334.9 1.0 copy.149
  336.0 1.0 copy.150
  337.0 1.0 copy.151
  338.0 2.2 copy.152
  340.3 1.0 copy.147
  341.3 2.9 slice.148
  344.2 0.6 copy-done.3
  344.8 1.0 slice.151
  345.9 0.6 copy-done.1
  346.5 7.8 %subtract_convert_fusion = bf16[16,256,512]{2,1,0:T(8,128)(2,1)} fusion(bf16[16,256,512]{2,1,0:T(8,128)(2,1)} %param.9, bf16[16,256,512]{1,2,0:T(8,128)(2,1)S(1)} %copy-done.1, bf16[16,128,128]{2,1,0:T(8,128)(2,1)} %get-tuple-element.7, bf16[16,128,128]{2,1,0:T(8,128)(2,1)} %bitcast.39, bf16[16,128,128]{2,1,0:T(8,128)(2,1)} %bitcast.38, ...), kind=kOutput, calls=%fused_computation.27 | convolution fusion | flops 2241855488 | bytes 20971520 | tf_op jit(solution)/shard_map/srf,sfg->srg/dot_general | solution.py:95
  (48 shorter events, 0.7 us)
Async XLA Ops:
  7.2 7.9 %copy-start.5 = (f32[16,256,64]{1,2,0:T(8,128)S(1)}, f32[16,256,64]{1,2,0:T(8,128)}, u32[]{:S(2)}) copy-start(f32[16,256,64]{1,2,0:T(8,128)} %param.11) | copy-start | bytes 3145732
  7.2 88.0 %all-reduce.2.cloned.1.call-start = ((), (), s32[]{:S(2)}) async-start(), calls=%async_computation.1 | async-start | bytes 2097152 | tf_op jit(solution)/shard_map/psum | solution.py:80
  7.2 7.8 %copy-start.2 = (bf16[16,256,512]{2,1,0:T(8,128)(2,1)S(1)}, bf16[16,256,512]{2,1,0:T(8,128)(2,1)}, u32[]{:S(2)}) copy-start(bf16[16,256,512]{2,1,0:T(8,128)(2,1)} %param.10) | copy-start | bytes 12582916
  16.9 6.5 %copy-start.13 = (s32[1,32]{1,0:T(1,128)S(1)}, s32[1,32]{1,0:T(1,128)}, u32[]{:S(2)}) copy-start(s32[1,32]{1,0:T(1,128)} %param.6) | copy-start | bytes 388
  16.9 205.0 %reduce-scatter.2.cloned.1.call-start = ((), (), s32[]{:S(2)}) async-start(), calls=%async_computation.2 | async-start | bytes 5898240 | tf_op jit(solution)/shard_map/reduce_scatter | solution.py:90
  29.6 6.5 %copy-start.14 = (s32[16]{0:T(128)S(1)}, s32[16]{0:T(128)}, u32[]{:S(2)}) copy-start(s32[16]{0:T(128)} %param.7) | copy-start | bytes 196
  101.6 5.6 %copy-start = (bf16[16,256,512]{1,2,0:T(8,128)(2,1)}, bf16[16,256,512]{1,2,0:T(8,128)(2,1)S(1)}, u32[]{:S(2)}) copy-start(bf16[16,256,512]{1,2,0:T(8,128)(2,1)S(1)} %fusion.21) | copy-start | bytes 12582916
  119.3 211.1 %all-gather.2.cloned.1.call-start = ((), (), s32[]{:S(2)}) async-start(), calls=%async_computation.3 | async-start | bytes 5898240 | tf_op jit(solution)/shard_map/all_gather | solution.py:93
  221.9 6.3 %copy-start.4 = (bf16[2,128,1280]{1,2,0:T(8,128)(2,1)S(1)}, bf16[2,128,1280]{1,2,0:T(8,128)(2,1)}, u32[]{:S(2)}) copy-start(bf16[2,128,1280]{1,2,0:T(8,128)(2,1)} %reduce-scatter.2.cloned.1.call-done) | copy-start | bytes 1966084
  224.5 3.9 %copy-start.6 = (f32[2,128,128]{1,2,0:T(8,128)S(1)}, f32[2,128,128]{1,2,0:T(8,128)}, u32[]{:S(2)}) copy-start(f32[2,128,128]{1,2,0:T(8,128)} %get-tuple-element.15) | copy-start | bytes 393220
  225.3 3.1 copy-start.7
  226.0 2.4 copy-start.8
  226.8 1.6 copy-start.9
  227.5 0.9 copy-start.10
  228.2 0.9 copy-start.11
  228.3 1.0 copy-start.12
  338.0 7.8 %slice-start = ((bf16[16,128,1280]{2,1,0:T(8,128)(2,1)}), bf16[16,128,512]{2,1,0:T(8,128)(2,1)S(1)}, s32[]{:S(2)}) async-start(bf16[16,128,1280]{2,1,0:T(8,128)(2,1)} %all-gather.2.cloned.1.call-done), calls=%async_computation.4 | async-start | bytes 4194304 | tf_op jit(solution)/shard_map/slice | solution.py:38
  341.3 3.5 copy-start.3
  341.3 5.2 %copy-start.1 = (bf16[16,256,512]{1,2,0:T(8,128)(2,1)S(1)}, bf16[16,256,512]{1,2,0:T(8,128)(2,1)}, u32[]{:S(2)}) copy-start(bf16[16,256,512]{1,2,0:T(8,128)(2,1)} %copy-done) | copy-start | bytes 12582916
Sparse Core Ops, SparseCore 0:
  17.0 78.1 all-reduce.1
  119.4 102.4 reduce-scatter.1
  245.4 84.9 all-gather.1

commit v2 on v1

v2 whole, which is shorter than its diff:
```python
import functools
import math

import jax
import jax.numpy as jnp
from jax import lax
from jax.experimental import pallas as pl
from jax.experimental.pallas import tpu as pltpu
from jax.sharding import PartitionSpec as P

D = 2048
FF = 512
ITERS = 3


momentum_decay = 0.9
residual_weight = 2.0
step_rate = 0.5
decay_rate = 0.1
coef_first = 3.4445
coef_second = -4.775
coef_third = 2.0315
epsilon = 1e-07
TILE = 128
MESH = pl.DeviceIdType.MESH
F32 = jnp.float32
BF16 = jnp.bfloat16


def grid_of(owners):
    inner = 2 if owners % 2 == 0 and owners <= 8 else 4
    return owners // inner, inner


class Plan:
    def __init__(self, owners):
        self.outer, self.inner = grid_of(owners)
        me = lax.axis_index("row")
        self.o = me // self.inner
        self.i = lax.rem(me, self.inner)

    def o_at(self, d):
        return lax.rem(self.o + d, self.outer)

    def i_at(self, d):
        return lax.rem(self.i + d, self.inner)

    def row(self, o, i):
        return o * self.inner + i

    def barrier(self):
        sem = pltpu.get_barrier_semaphore()
        for d in range(1, self.inner):
            pl.semaphore_signal(
                sem, inc=1, device_id={"row": self.row(self.o, self.i_at(d))}, device_id_type=MESH
            )
        for d in range(1, self.outer):
            pl.semaphore_signal(
                sem, inc=1, device_id={"row": self.row(self.o_at(d), self.i)}, device_id_type=MESH
            )
        pl.semaphore_wait(sem, self.inner + self.outer - 2)


def remote(src, dst, send, recv, target):
    return pltpu.make_async_remote_copy(
        src_ref=src,
        dst_ref=dst,
        send_sem=send,
        recv_sem=recv,
        device_id={"row": target},
        device_id_type=MESH,
    )


class SumScatter:
    def __init__(self, plan, per, x, near, far, sums, sems):
        self.plan, self.per, self.x, self.near, self.far, self.sums = plan, per, x, near, far, sums
        self.s1, self.r1, self.s2, self.r2 = sems
        self.second = {}

    @staticmethod
    def scratch(owners, per, tile):
        outer, inner = grid_of(owners)
        dma = pltpu.SemaphoreType.DMA
        return [
            pltpu.VMEM((inner - 1, outer, per) + tile, BF16),
            pltpu.VMEM((outer - 1, per) + tile, BF16),
            pltpu.VMEM((outer, per) + tile, BF16),
            dma((inner - 1, outer, per)),
            dma((inner - 1, outer, per)),
            dma((outer - 1, per)),
            dma((outer - 1, per)),
        ]

    def steps(self):
        return [(p, d) for p in range(self.per) for d in list(range(1, self.plan.outer)) + [0]]

    def first_copy(self, p, d, e):
        plan = self.plan
        target = plan.row(plan.o, plan.i_at(e))
        return remote(
            self.x.at[plan.row(plan.o_at(d), plan.i_at(e)) * self.per + p],
            self.near.at[e - 1, d, p],
            self.s1.at[e - 1, d, p],
            self.r1.at[e - 1, d, p],
            target,
        )

    def start(self):
        for p, d in self.steps():
            for e in range(1, self.plan.inner):
                self.first_copy(p, d, e).start()

    def partial(self, p, d):
        plan = self.plan
        total = self.x[plan.row(plan.o_at(d), plan.i) * self.per + p].astype(F32)
        for e in range(1, plan.inner):
            self.first_copy(p, d, e).wait_recv()
            total = total + self.near[e - 1, d, p].astype(F32)
        return total

    def second_copy(self, p, d):
        plan = self.plan
        return remote(
            self.sums.at[d, p],
            self.far.at[d - 1, p],
            self.s2.at[d - 1, p],
            self.r2.at[d - 1, p],
            plan.row(plan.o_at(d), plan.i),
        )

    def forward(self, p):
        for d in range(1, self.plan.outer):
            self.sums[d, p] = self.partial(p, d).astype(BF16)
            self.second_copy(p, d).start()
        self.sums[0, p] = self.partial(p, 0).astype(BF16)

    def total(self, p):
        value = self.sums[0, p].astype(F32)
        for d in range(1, self.plan.outer):
            self.second_copy(p, d).wait_recv()
            value = value + self.far[d - 1, p].astype(F32)
        return value

    def finish(self):
        for p, d in self.steps():
            for e in range(1, self.plan.inner):
                self.first_copy(p, d, e).wait_send()
            if d:
                self.second_copy(p, d).wait_send()


class Gather:
    def __init__(self, plan, per, out, sems):
        self.plan, self.per, self.out = plan, per, out
        self.s1, self.r1, self.s2, self.r2 = sems

    @staticmethod
    def scratch(owners, per):
        outer, inner = grid_of(owners)
        dma = pltpu.SemaphoreType.DMA
        return [
            dma((outer - 1, per)),
            dma((outer - 1, per)),
            dma((inner - 1, outer, per)),
            dma((inner - 1, outer, per)),
        ]

    def place(self, o, p):
        return self.out.at[self.plan.row(o, self.plan.i) * self.per + p]

    def first_copy(self, p, d):
        plan = self.plan
        own = self.place(plan.o, p)
        return remote(own, own, self.s1.at[d - 1, p], self.r1.at[d - 1, p], plan.row(plan.o_at(d), plan.i))

    def second_copy(self, p, d, e):
        plan = self.plan
        own = self.place(plan.o_at(plan.outer - d), p)
        return remote(
            own, own, self.s2.at[e - 1, d, p], self.r2.at[e - 1, d, p], plan.row(plan.o, plan.i_at(e))
        )

    def start(self, p, value):
        plan = self.plan
        self.out[plan.row(plan.o, plan.i) * self.per + p] = value
        for d in range(1, plan.outer):
            self.first_copy(p, d).start()
        for e in range(1, plan.inner):
            self.second_copy(p, 0, e).start()

    def forward(self, p):
        plan = self.plan
        for d in range(1, plan.outer):
            self.first_copy(p, d).wait_recv()
            for e in range(1, plan.inner):
                self.second_copy(p, d, e).start()

    def finish(self):
        plan = self.plan
        for p in range(self.per):
            for d in range(1, plan.outer):
                self.first_copy(p, d).wait_send()
            for d in range(plan.outer):
                for e in range(1, plan.inner):
                    copy = self.second_copy(p, d, e)
                    copy.wait_recv()
                    copy.wait_send()


def sum_kernel(owners, per, x, out, *scratch):
    plan = Plan(owners)
    plan.barrier()
    scatter = SumScatter(plan, per, x, *scratch[:3], scratch[3:7])
    gather = Gather(plan, per, out, scratch[7:])
    scatter.start()
    for p in range(per):
        scatter.forward(p)
    for p in range(per):
        gather.start(p, scatter.total(p).astype(BF16))
    for p in range(per):
        gather.forward(p)
    scatter.finish()
    gather.finish()


def vmem():
    return pl.BlockSpec(memory_space=pltpu.VMEM)


def all_sum(x, owners, collective_id):
    per = x.shape[0] // owners
    return pl.pallas_call(
        functools.partial(sum_kernel, owners, per),
        out_shape=jax.ShapeDtypeStruct(x.shape, x.dtype),
        in_specs=[vmem()],
        out_specs=vmem(),
        scratch_shapes=SumScatter.scratch(owners, per, x.shape[1:]) + Gather.scratch(owners, per),
        compiler_params=pltpu.CompilerParams(
            collective_id=collective_id, has_side_effects=True, vmem_limit_bytes=20 << 20
        ),
        name="proj_sum",
    )(x)


def unpack_upper(packed, width):
    count = width // TILE
    tiles = {}
    offset = 0
    for i in range(count):
        for j in range(i, count):
            tile = packed[:, offset : offset + TILE]
            tiles[i, j] = tile
            if j > i:
                tiles[j, i] = tile.T
            offset += TILE
    return jnp.concatenate(
        [jnp.concatenate([tiles[i, j] for j in range(count)], axis=1) for i in range(count)], axis=0
    )


def pack_upper(full):
    width = full.shape[-1]
    return jnp.concatenate([full[at : at + TILE, at:] for at in range(0, width, TILE)], axis=1)


def mm(a, b):
    return jnp.dot(a.astype(BF16), b.astype(BF16), preferred_element_type=F32)


def factors(gram):
    width = gram.shape[-1]
    rows = lax.broadcasted_iota(jnp.int32, (width, width), 0)
    columns = lax.broadcasted_iota(jnp.int32, (width, width), 1)
    diagonal = rows == columns
    first_eye = jnp.where(diagonal, coef_first, 0.0)
    squares = jnp.sum(jnp.where(diagonal, gram, 0.0), axis=0, keepdims=True)
    total = jnp.sum(squares, axis=1, keepdims=True)
    inverse = 1.0 / (jnp.sqrt(total) + epsilon)
    a = gram * inverse * inverse
    q = None
    for sweep in range(ITERS):
        poly = coef_second * a + coef_third * mm(a, a)
        q = first_eye + poly if q is None else coef_first * q + mm(q, poly)
        if sweep < ITERS - 1:
            half = coef_first * a + mm(a, poly)
            a = coef_first * half + mm(poly, half)
    return q * inverse


def gram_kernel(owners, per, width, x, out, *scratch):
    plan = Plan(owners)
    plan.barrier()
    scatter = SumScatter(plan, per, x, *scratch[:3], scratch[3:7])
    gather = Gather(plan, per, out, scratch[7:])
    scatter.start()
    for p in range(per):
        scatter.forward(p)
    for p in range(per):
        gather.start(p, pack_upper(factors(unpack_upper(scatter.total(p), width)).astype(BF16)))
    for p in range(per):
        gather.forward(p)
    scatter.finish()
    gather.finish()


def gram_factors(x, owners, width, collective_id):
    per = x.shape[0] // owners
    return pl.pallas_call(
        functools.partial(gram_kernel, owners, per, width),
        out_shape=jax.ShapeDtypeStruct(x.shape, x.dtype),
        in_specs=[vmem()],
        out_specs=vmem(),
        scratch_shapes=SumScatter.scratch(owners, per, x.shape[1:]) + Gather.scratch(owners, per),
        compiler_params=pltpu.CompilerParams(
            collective_id=collective_id, has_side_effects=True, vmem_limit_bytes=50 << 20
        ),
        name="gram_factors",
    )(x)


def momentum_kernel(count, chosen, flags, bank, grad, basis, proj, new_bank, mom, gram):
    step = pl.program_id(0)

    @pl.when(step < count)
    def _():
        low = lax.dot_general(
            basis[0].astype(BF16), proj[0], (((0,), (0,)), ((), ())), preferred_element_type=F32
        )
        flag = residual_weight * flags[jnp.minimum(step, count - 1)].astype(F32)
        fresh = (
            momentum_decay * bank[0].astype(F32) + low + flag * (grad[0].astype(F32) - low)
        ).astype(BF16)
        new_bank[0] = fresh
        mom[0] = fresh
        width = fresh.shape[1]
        offset = 0
        for at in range(0, width, TILE):
            block = lax.dot_general(
                fresh[:, at : at + TILE],
                fresh[:, at:],
                (((0,), (0,)), ((), ())),
                preferred_element_type=F32,
            )
            gram[0, :, offset : offset + width - at] = block.astype(BF16)
            offset += width - at

    @pl.when(step >= count)
    def _():
        new_bank[0] = bank[0]


def momentum(order, refresh, bank, grads, basis_t, proj):
    count, rows, width = grads.shape
    tiles = width // TILE
    packed = TILE * (tiles * (tiles + 1) // 2)
    rank = basis_t.shape[1]

    def by_expert(step, chosen, flags):
        return (chosen[step], 0, 0)

    def by_sample(step, chosen, flags):
        return (jnp.minimum(step, count - 1), 0, 0)

    return pl.pallas_call(
        functools.partial(momentum_kernel, count),
        out_shape=(
            jax.ShapeDtypeStruct(bank.shape, bank.dtype),
            jax.ShapeDtypeStruct(grads.shape, BF16),
            jax.ShapeDtypeStruct((count, TILE, packed), BF16),
        ),
        grid_spec=pltpu.PrefetchScalarGridSpec(
            num_scalar_prefetch=2,
            grid=(bank.shape[0],),
            in_specs=[
                pl.BlockSpec((1, rows, width), by_expert),
                pl.BlockSpec((1, rows, width), by_sample),
                pl.BlockSpec((1, rank, rows), by_sample),
                pl.BlockSpec((1, rank, width), by_sample),
            ],
            out_specs=[
                pl.BlockSpec((1, rows, width), by_expert),
                pl.BlockSpec((1, rows, width), by_sample),
                pl.BlockSpec((1, TILE, packed), by_sample),
            ],
        ),
        compiler_params=pltpu.CompilerParams(dimension_semantics=("arbitrary",)),
        name="momentum",
    )(order, refresh, bank, grads, basis_t, proj)


def weights_kernel(weights, mom, packed, out):
    scale_step = step_rate * 0.2 * math.sqrt(max(D, FF))
    full = unpack_upper(packed[0], mom.shape[2])
    ortho = jnp.dot(mom[0], full, preferred_element_type=F32)
    kept = weights[0].astype(F32) * (1.0 - step_rate * decay_rate)
    out[0] = (kept - scale_step * ortho).astype(BF16)


def update_weights(weights, mom, packed):
    def block(array):
        return pl.BlockSpec((1,) + array.shape[1:], lambda step: (step, 0, 0))

    return pl.pallas_call(
        weights_kernel,
        out_shape=jax.ShapeDtypeStruct(weights.shape, weights.dtype),
        grid=(weights.shape[0],),
        in_specs=[block(weights), block(mom), block(packed)],
        out_specs=block(weights),
        compiler_params=pltpu.CompilerParams(dimension_semantics=("arbitrary",)),
        name="update_weights",
    )(weights, mom, packed)


def shards(owners, sampled, refresh, momentum_bank, weights, grads, basis):
    width = weights.shape[2]
    basis_t = jnp.swapaxes(basis, 1, 2)
    partial_sum = jnp.einsum(
        "skr,srf->skf", basis_t.astype(BF16), grads, preferred_element_type=F32
    )
    proj = all_sum(partial_sum.astype(BF16), owners, 0)
    new_bank, mom, gram = momentum(sampled[0], refresh, momentum_bank, grads, basis_t, proj)
    packed = gram_factors(gram, owners, width, 1)
    return new_bank, update_weights(weights, mom, packed)


def solution(mesh):
    in_specs = (
        P("expert", None),
        P("expert"),
        P("expert", "row", None),
        P("expert", "row", None),
        P("expert", "row", None),
        P("expert", "row", None),
    )
    out_specs = (P("expert", "row", None), P("expert", "row", None))
    return jax.shard_map(
        functools.partial(shards, mesh.shape["row"]),
        mesh=mesh,
        in_specs=in_specs,
        out_specs=out_specs,
        check_vma=False,
    )
```

time: 365 us -> 232 us (0.64)
  waiting for transfers between devices: 229 us -> 0 us
  Pallas kernels: 0 us -> 225 us
  local copies, waits for them, and re-layouts: 74.6 us -> 0.96 us
  matrix products: 36 us -> 3.35 us
  between operations: 14 us -> 0.66 us
  other arithmetic: 6.96 us -> 0 us
    pallas_call x0 -> x4, Pallas kernels: none -> 225 us  [the longest x1 149 us: gram_factors(): pl.pallas_call(functools.partial(gram_kernel, owners, per, width), out_sh...]
    reduce_scatter x1 -> x0, waiting for transfers between devices: 102 us -> none  [shards(): summed = lax.psum_scatter(packed, 'row', scatter_dimension=0, tiled=True)]
    all_gather x1 -> x0, waiting for transfers between devices: 67.6 us -> none  [shards(): everyone = lax.all_gather(sent, 'row', axis=0, tiled=True)]
    psum x1 -> x0, waiting for transfers between devices: 59.1 us -> none  [shards(): proj = lax.psum(partial_sum.astype(jnp.bfloat16), 'row')]
    dot_general x12 -> x1, matrix products: 36 us -> 3.35 us  [shards(): jnp.einsum('skr,srf->skf', basis_t.astype(BF16), grads, preferred_element...]
    unnamed x44 -> x2, local copies, waits for them, and re-layouts: 28.1 us -> 0.96 us
    slice x17 -> x0, local copies, waits for them, and re-layouts: 15.2 us -> none  [the longest x9 9.41 us: unpack_upper(): tile = packed[:, :, offset:offset + TILE]]
    gather x2 -> x0, local copies, waits for them, and re-layouts: 12.7 us -> none  [shards(): old = momentum_bank[chosen].astype(jnp.float32)]
  transfers between devices with their start and end apart: 3 -> 0, of which waited for: 3 -> 0; matrix products, arithmetic and copies ran while one was open for 10% -> 0% of each run, Pallas kernels for 0% -> 0%
where the time goes in v2:
time: 232 us; the launch traced here: 230 us
  Pallas kernels  225 us (97%)
  matrix products  3.35 us (1%)
    pallas_call x1, Pallas kernels, gram_factors(): pl.pallas_call(functools.partial(gram_kernel, owners, per, width), out_sh...  149 us
    pallas_call x1, Pallas kernels, all_sum(): pl.pallas_call(functools.partial(sum_kernel, owners, per), out_shape=jax....  35.2 us
    pallas_call x1, Pallas kernels, momentum(): pl.pallas_call(functools.partial(momentum_kernel, count), out_shape=(jax....  26.7 us
    pallas_call x1, Pallas kernels, update_weights(): pl.pallas_call(weights_kernel, out_shape=jax.ShapeDtypeStruct(weights.sha...  14.2 us

profile of v2, /device:TPU:24, one launch (start us, length us, event | category | flops | bytes accessed | tf_op | source)
XLA Modules:
  0.0 230.4 jit_solution(13280295109158351736)
XLA Ops:
  0.6 3.4 %fusion.3.x = bf16[16,64,512]{2,1,0:T(8,128)(2,1)S(1)} fusion(bf16[16,256,512]{2,1,0:T(8,128)(2,1)} %grad.1, f32[16,256,64]{1,2,0:T(8,128)} %param.11), kind=kOutput, calls=%fused_computation.3 | convolution fusion | flops 268435456 | bytes 6291456 | tf_op jit(solution)/shard_map/skr,srf->skf/dot_general | solution.py:418
  4.0 35.2 %proj_sum.1.proj = bf16[16,64,512]{2,1,0:T(8,128)(2,1)S(1)} custom-call(bf16[16,64,512]{2,1,0:T(8,128)(2,1)S(1)} %fusion.3.x), custom_call_target="tpu_custom_call" | custom-call | tf_op jit(solution)/shard_map/proj_sum/pallas_call | solution.py:233
  39.1 0.0 copy-start
  39.2 1.0 copy-done
  40.1 26.7 %momentum.1 = (bf16[32,256,512]{2,1,0:T(8,128)(2,1)}, bf16[16,256,512]{2,1,0:T(8,128)(2,1)}, bf16[16,128,1280]{2,1,0:T(8,128)(2,1)}) custom-call(s32[32]{0:T(128)} %bitcast.17, s32[16]{0:T(128)} %flags.1, bf16[32,256,512]{2,1,0:T(8,128)(2,1)} %bank.1, bf16[16,256,512]{2,1,0:T(8,128)(2,1)} %grad.1, f32[16,64,256]{2,1,0:T(8,128)} %bitcast.16, ...), custom_call_target="tpu_custom_call" | custom-call | tf_op jit(solution)/shard_map/momentum/pallas_call | solution.py:365
  66.9 149.3 %gram_factors.1.packed = bf16[16,128,1280]{2,1,0:T(8,128)(2,1)} custom-call(bf16[16,128,1280]{2,1,0:T(8,128)(2,1)} %get-tuple-element.7.x), custom_call_target="tpu_custom_call" | custom-call | tf_op jit(solution)/shard_map/gram_factors/pallas_call | solution.py:309
  216.2 14.2 %update_weights.1 = bf16[16,256,512]{2,1,0:T(8,128)(2,1)} custom-call(bf16[16,256,512]{2,1,0:T(8,128)(2,1)} %weights.1, bf16[16,256,512]{2,1,0:T(8,128)(2,1)} %get-tuple-element.6.mom, bf16[16,128,1280]{2,1,0:T(8,128)(2,1)} %gram_factors.1.packed), custom_call_target="tpu_custom_call" | custom-call | tf_op jit(solution)/shard_map/update_weights/pallas_call | solution.py:404
Async XLA Ops:
  39.1 1.0 copy-start

commit v3 on v2

--- a/solution.py
+++ b/solution.py
@@ -22,6 +22,7 @@
 coef_third = 2.0315
 epsilon = 1e-07
 TILE = 128
+GRANT = 34 << 20
 MESH = pl.DeviceIdType.MESH
 F32 = jnp.float32
 BF16 = jnp.bfloat16
@@ -129,11 +130,15 @@
             plan.row(plan.o_at(d), plan.i),
         )
 
+    def forward_one(self, p, d):
+        self.sums[d, p] = self.partial(p, d).astype(BF16)
+        if d:
+            self.second_copy(p, d).start()
+
     def forward(self, p):
-        for d in range(1, self.plan.outer):
-            self.sums[d, p] = self.partial(p, d).astype(BF16)
-            self.second_copy(p, d).start()
-        self.sums[0, p] = self.partial(p, 0).astype(BF16)
+        for q, d in self.steps():
+            if q == p:
+                self.forward_one(p, d)
 
     def total(self, p):
         value = self.sums[0, p].astype(F32)
@@ -181,9 +186,11 @@
             own, own, self.s2.at[e - 1, d, p], self.r2.at[e - 1, d, p], plan.row(plan.o, plan.i_at(e))
         )
 
-    def start(self, p, value):
-        plan = self.plan
-        self.out[plan.row(plan.o, plan.i) * self.per + p] = value
+    def mine(self, p):
+        return self.plan.row(self.plan.o, self.plan.i) * self.per + p
+
+    def start(self, p):
+        plan = self.plan
         for d in range(1, plan.outer):
             self.first_copy(p, d).start()
         for e in range(1, plan.inner):
@@ -195,6 +202,14 @@
             self.first_copy(p, d).wait_recv()
             for e in range(1, plan.inner):
                 self.second_copy(p, d, e).start()
+
+    def arrive(self, p, d):
+        plan = self.plan
+        places = []
+        for e in range(1, plan.inner):
+            self.second_copy(p, d, e).wait_recv()
+            places.append(plan.row(plan.o_at(plan.outer - d), plan.i_at(plan.inner - e)) * self.per + p)
+        return places
 
     def finish(self):
         plan = self.plan
@@ -203,9 +218,7 @@
                 self.first_copy(p, d).wait_send()
             for d in range(plan.outer):
                 for e in range(1, plan.inner):
-                    copy = self.second_copy(p, d, e)
-                    copy.wait_recv()
-                    copy.wait_send()
+                    self.second_copy(p, d, e).wait_send()
 
 
 def sum_kernel(owners, per, x, out, *scratch):
@@ -217,9 +230,13 @@
     for p in range(per):
         scatter.forward(p)
     for p in range(per):
-        gather.start(p, scatter.total(p).astype(BF16))
+        out[gather.mine(p)] = scatter.total(p).astype(BF16)
+        gather.start(p)
     for p in range(per):
         gather.forward(p)
+    for p in range(per):
+        for d in range(plan.outer):
+            gather.arrive(p, d)
     scatter.finish()
     gather.finish()
 
@@ -243,25 +260,71 @@
     )(x)
 
 
-def unpack_upper(packed, width):
+def triangle():
+    rows = lax.broadcasted_iota(jnp.int32, (TILE, TILE), 0)
+    columns = lax.broadcasted_iota(jnp.int32, (TILE, TILE), 1)
+    return rows, columns
+
+
+def pairs(count):
+    return [(i, j) for i in range(count) for j in range(i + 1, count)]
+
+
+EXTRA = 16
+
+
+def packed_rows(width):
     count = width // TILE
+    return TILE * (len(pairs(count)) + count // 2) + EXTRA
+
+
+def pack(tile):
+    count = tile.count
+    rows, columns = triangle()
+    at = 0
+    for i, j in pairs(count):
+        yield at, tile(i, j).astype(BF16)
+        at += TILE
+    extra = lax.broadcasted_iota(jnp.int32, (EXTRA, TILE), 0)
+    diagonals = jnp.zeros((EXTRA, TILE), F32)
+    for k in range(0, count, 2):
+        upper, lower = tile(k, k), tile(k + 1, k + 1)
+        yield at, jnp.where(rows <= columns, upper, lower).astype(BF16)
+        at += TILE
+        diagonal = jnp.sum(jnp.where(rows == columns, lower, 0.0), axis=0, keepdims=True)
+        diagonals = jnp.where(extra == k // 2, diagonal, diagonals)
+    yield at, diagonals.astype(BF16)
+
+
+class Tiles:
+    def __init__(self, count, get):
+        self.count, self.get = count, get
+
+    def __call__(self, i, j):
+        return self.get(i, j)
+
+
+def unpack(packed, width, dtype):
+    count = width // TILE
+    rows, columns = triangle()
     tiles = {}
-    offset = 0
-    for i in range(count):
-        for j in range(i, count):
-            tile = packed[:, offset : offset + TILE]
-            tiles[i, j] = tile
-            if j > i:
-                tiles[j, i] = tile.T
-            offset += TILE
+    at = 0
+    for i, j in pairs(count):
+        tile = packed[at : at + TILE].astype(dtype)
+        tiles[i, j], tiles[j, i] = tile, tile.T
+        at += TILE
+    diagonals = packed[at + TILE * (count // 2) :].astype(F32)
+    for k in range(0, count, 2):
+        both = packed[at : at + TILE].astype(F32)
+        other = both.T
+        line = diagonals[k // 2 : k // 2 + 1]
+        tiles[k, k] = jnp.where(rows <= columns, both, other).astype(dtype)
+        lower = jnp.where(rows > columns, both, other)
+        tiles[k + 1, k + 1] = jnp.where(rows == columns, line, lower).astype(dtype)
+        at += TILE
     return jnp.concatenate(
         [jnp.concatenate([tiles[i, j] for j in range(count)], axis=1) for i in range(count)], axis=0
     )
-
-
-def pack_upper(full):
-    width = full.shape[-1]
-    return jnp.concatenate([full[at : at + TILE, at:] for at in range(0, width, TILE)], axis=1)
 
 
 def mm(a, b):
@@ -288,38 +351,113 @@
     return q * inverse
 
 
-def gram_kernel(owners, per, width, x, out, *scratch):
+def store_gram(mom, s, x):
+    fresh = mom[s]
+    width = fresh.shape[1]
+    lines = {}
+
+    def tile(i, j):
+        if i not in lines:
+            lines[i] = lax.dot_general(
+                fresh[:, i * TILE : (i + 1) * TILE],
+                fresh[:, i * TILE :],
+                (((0,), (0,)), ((), ())),
+                preferred_element_type=F32,
+            )
+        return lines[i][:, (j - i) * TILE : (j - i + 1) * TILE]
+
+    for at, piece in pack(Tiles(width // TILE, tile)):
+        x[s, at : at + piece.shape[0]] = piece
+
+
+def store_factors(value, width, s, out):
+    q = factors(unpack(value, width, F32))
+
+    def tile(i, j):
+        return q[i * TILE : (i + 1) * TILE, j * TILE : (j + 1) * TILE]
+
+    for at, piece in pack(Tiles(width // TILE, tile)):
+        out[s, at : at + piece.shape[0]] = piece
+
+
+def store_weights(weights, mom, packed, s, out):
+    scale_step = step_rate * 0.2 * math.sqrt(max(D, FF))
+    full = unpack(packed[s], mom.shape[2], BF16)
+    ortho = jnp.dot(mom[s], full, preferred_element_type=F32)
+    kept = weights[s].astype(F32) * (1.0 - step_rate * decay_rate)
+    out[s] = (kept - scale_step * ortho).astype(BF16)
+
+
+def gram_kernel(owners, per, mom, weights, out, x, packed, *scratch):
+    width = mom.shape[2]
     plan = Plan(owners)
     plan.barrier()
     scatter = SumScatter(plan, per, x, *scratch[:3], scratch[3:7])
-    gather = Gather(plan, per, out, scratch[7:])
-    scatter.start()
-    for p in range(per):
-        scatter.forward(p)
-    for p in range(per):
-        gather.start(p, pack_upper(factors(unpack_upper(scatter.total(p), width)).astype(BF16)))
-    for p in range(per):
-        gather.forward(p)
+    gather = Gather(plan, per, packed, scratch[7:])
+    outer, inner = plan.outer, plan.inner
+
+    def first(p):
+        @pl.loop(1, outer + 1)
+        def _(later):
+            d = lax.rem(later, outer)
+            for e in range(1, inner):
+                store_gram(mom, plan.row(plan.o_at(d), plan.i_at(e)) * per + p, x)
+                scatter.first_copy(p, d, e).start()
+
+    def own(p):
+        @pl.loop(0, outer)
+        def _(d):
+            store_gram(mom, plan.row(plan.o_at(d), plan.i) * per + p, x)
+
+    def owner_work(p):
+        store_factors(scatter.total(p), width, gather.mine(p), packed)
+        gather.start(p)
+
+    def last(p):
+        for d in range(outer):
+            store_weights(weights, mom, packed, plan.row(plan.o_at(outer - d), plan.i) * per + p, out)
+            for s in gather.arrive(p, d):
+                store_weights(weights, mom, packed, s, out)
+
+    for p in range(per):
+        first(p)
+        own(p)
+    scatter.forward(0)
+    for p in range(per):
+        if p + 1 < per:
+            scatter.forward_one(p + 1, 1)
+        owner_work(p)
+        if p + 1 < per:
+            for d in list(range(2, outer)) + [0]:
+                scatter.forward_one(p + 1, d)
+            gather.forward(p)
+    gather.forward(per - 1)
+    for p in range(per):
+        last(p)
     scatter.finish()
     gather.finish()
 
 
-def gram_factors(x, owners, width, collective_id):
-    per = x.shape[0] // owners
+def gram_update(mom, weights, owners, collective_id):
+    count, rows, width = mom.shape
+    per = count // owners
+    tile = (packed_rows(width), TILE)
     return pl.pallas_call(
-        functools.partial(gram_kernel, owners, per, width),
-        out_shape=jax.ShapeDtypeStruct(x.shape, x.dtype),
-        in_specs=[vmem()],
+        functools.partial(gram_kernel, owners, per),
+        out_shape=jax.ShapeDtypeStruct(weights.shape, weights.dtype),
+        in_specs=[vmem(), vmem()],
         out_specs=vmem(),
-        scratch_shapes=SumScatter.scratch(owners, per, x.shape[1:]) + Gather.scratch(owners, per),
+        scratch_shapes=[pltpu.VMEM((count,) + tile, BF16), pltpu.VMEM((count,) + tile, BF16)]
+        + SumScatter.scratch(owners, per, tile)
+        + Gather.scratch(owners, per),
         compiler_params=pltpu.CompilerParams(
-            collective_id=collective_id, has_side_effects=True, vmem_limit_bytes=50 << 20
+            collective_id=collective_id, has_side_effects=True, vmem_limit_bytes=GRANT
         ),
-        name="gram_factors",
-    )(x)
-
-
-def momentum_kernel(count, chosen, flags, bank, grad, basis, proj, new_bank, mom, gram):
+        name="gram_update",
+    )(mom, weights)
+
+
+def momentum_kernel(count, chosen, flags, bank, grad, basis, proj, new_bank, mom):
     step = pl.program_id(0)
 
     @pl.when(step < count)
@@ -333,17 +471,6 @@
         ).astype(BF16)
         new_bank[0] = fresh
         mom[0] = fresh
-        width = fresh.shape[1]
-        offset = 0
-        for at in range(0, width, TILE):
-            block = lax.dot_general(
-                fresh[:, at : at + TILE],
-                fresh[:, at:],
-                (((0,), (0,)), ((), ())),
-                preferred_element_type=F32,
-            )
-            gram[0, :, offset : offset + width - at] = block.astype(BF16)
-            offset += width - at
 
     @pl.when(step >= count)
     def _():
@@ -352,8 +479,6 @@
 
 def momentum(order, refresh, bank, grads, basis_t, proj):
     count, rows, width = grads.shape
-    tiles = width // TILE
-    packed = TILE * (tiles * (tiles + 1) // 2)
     rank = basis_t.shape[1]
 
     def by_expert(step, chosen, flags):
@@ -367,7 +492,6 @@
         out_shape=(
             jax.ShapeDtypeStruct(bank.shape, bank.dtype),
             jax.ShapeDtypeStruct(grads.shape, BF16),
-            jax.ShapeDtypeStruct((count, TILE, packed), BF16),
         ),
         grid_spec=pltpu.PrefetchScalarGridSpec(
             num_scalar_prefetch=2,
@@ -381,7 +505,6 @@
             out_specs=[
                 pl.BlockSpec((1, rows, width), by_expert),
                 pl.BlockSpec((1, rows, width), by_sample),
-                pl.BlockSpec((1, TILE, packed), by_sample),
             ],
         ),
         compiler_params=pltpu.CompilerParams(dimension_semantics=("arbitrary",)),
@@ -389,39 +512,14 @@
     )(order, refresh, bank, grads, basis_t, proj)
 
 
-def weights_kernel(weights, mom, packed, out):
-    scale_step = step_rate * 0.2 * math.sqrt(max(D, FF))
-    full = unpack_upper(packed[0], mom.shape[2])
-    ortho = jnp.dot(mom[0], full, preferred_element_type=F32)
-    kept = weights[0].astype(F32) * (1.0 - step_rate * decay_rate)
-    out[0] = (kept - scale_step * ortho).astype(BF16)
-
-
-def update_weights(weights, mom, packed):
-    def block(array):
-        return pl.BlockSpec((1,) + array.shape[1:], lambda step: (step, 0, 0))
-
-    return pl.pallas_call(
-        weights_kernel,
-        out_shape=jax.ShapeDtypeStruct(weights.shape, weights.dtype),
-        grid=(weights.shape[0],),
-        in_specs=[block(weights), block(mom), block(packed)],
-        out_specs=block(weights),
-        compiler_params=pltpu.CompilerParams(dimension_semantics=("arbitrary",)),
-        name="update_weights",
-    )(weights, mom, packed)
-
-
 def shards(owners, sampled, refresh, momentum_bank, weights, grads, basis):
-    width = weights.shape[2]
     basis_t = jnp.swapaxes(basis, 1, 2)
     partial_sum = jnp.einsum(
         "skr,srf->skf", basis_t.astype(BF16), grads, preferred_element_type=F32
     )
     proj = all_sum(partial_sum.astype(BF16), owners, 0)
-    new_bank, mom, gram = momentum(sampled[0], refresh, momentum_bank, grads, basis_t, proj)
-    packed = gram_factors(gram, owners, width, 1)
-    return new_bank, update_weights(weights, mom, packed)
+    new_bank, mom = momentum(sampled[0], refresh, momentum_bank, grads, basis_t, proj)
+    return new_bank, gram_update(mom, weights, owners, 1)
 
 
 def solution(mesh):

time: 232 us -> 191 us (0.82)
  Pallas kernels: 225 us -> 178 us
  local copies, waits for them, and re-layouts: 0.96 us -> 7.35 us
    pallas_call x2 -> x1, Pallas kernels: 164 us -> 119 us  [gram_update(): pl.pallas_call(functools.partial(gram_kernel, owners, per), out_shape=jax...]
    unnamed x2 -> x7, local copies, waits for them, and re-layouts: 0.96 us -> 7.35 us
    pallas_call x1, Pallas kernels: 26.7 us -> 23.7 us  [momentum(): pl.pallas_call(functools.partial(momentum_kernel, count), out_shape=(jax....]
where the time goes in v3:
time: 191 us; the launch traced here: 189 us
  Pallas kernels  178 us (93%)
  local copies, waits for them, and re-layouts  7.35 us (4%)
  matrix products  3.35 us (2%)
    pallas_call x1, Pallas kernels, gram_update(): pl.pallas_call(functools.partial(gram_kernel, owners, per), out_shape=jax...  119 us
    pallas_call x1, Pallas kernels, all_sum(): pl.pallas_call(functools.partial(sum_kernel, owners, per), out_shape=jax....  35.2 us
    pallas_call x1, Pallas kernels, momentum(): pl.pallas_call(functools.partial(momentum_kernel, count), out_shape=(jax....  23.7 us
    unnamed x7, local copies, waits for them, and re-layouts  7.35 us

profile of v3, /device:TPU:24, one launch (start us, length us, event | category | flops | bytes accessed | tf_op | source)
XLA Modules:
  0.0 189.2 jit_solution(11887016843937291303)
XLA Ops:
  0.6 3.4 %fusion.3.x = bf16[16,64,512]{2,1,0:T(8,128)(2,1)S(1)} fusion(bf16[16,256,512]{2,1,0:T(8,128)(2,1)} %grad.1, f32[16,256,64]{1,2,0:T(8,128)} %param.11), kind=kOutput, calls=%fused_computation.3 | convolution fusion | flops 268435456 | bytes 6291456 | tf_op jit(solution)/shard_map/skr,srf->skf/dot_general | solution.py:517
  4.0 35.2 %proj_sum.1.proj = bf16[16,64,512]{2,1,0:T(8,128)(2,1)S(1)} custom-call(bf16[16,64,512]{2,1,0:T(8,128)(2,1)S(1)} %fusion.3.x), custom_call_target="tpu_custom_call" | custom-call | tf_op jit(solution)/shard_map/proj_sum/pallas_call | solution.py:250
  39.2 0.0 copy-start.2
  39.2 1.0 copy-done.2
  40.2 23.7 %momentum.1 = (bf16[32,256,512]{2,1,0:T(8,128)(2,1)}, bf16[16,256,512]{2,1,0:T(8,128)(2,1)}) custom-call(s32[32]{0:T(128)} %bitcast.17, s32[16]{0:T(128)} %flags.1, bf16[32,256,512]{2,1,0:T(8,128)(2,1)} %bank.1, bf16[16,256,512]{2,1,0:T(8,128)(2,1)} %grad.1, f32[16,64,256]{2,1,0:T(8,128)} %bitcast.16, bf16[16,64,512]{2,1,0:T(8,128)(2,1)} %copy-done.2), custom_call_target="tpu_custom_call" | custom-call | tf_op jit(solution)/shard_map/momentum/pallas_call | solution.py:490
  63.9 0.0 copy-start
  63.9 2.2 %copy-done = bf16[16,256,512]{2,1,0:T(8,128)(2,1)S(1)} copy-done((bf16[16,256,512]{2,1,0:T(8,128)(2,1)S(1)}, bf16[16,256,512]{2,1,0:T(8,128)(2,1)}, u32[]{:S(2)}) %copy-start) | copy-done | bytes 4194328
  66.0 0.0 copy-start.1
  66.0 2.2 %copy-done.1 = bf16[16,256,512]{2,1,0:T(8,128)(2,1)S(1)} copy-done((bf16[16,256,512]{2,1,0:T(8,128)(2,1)S(1)}, bf16[16,256,512]{2,1,0:T(8,128)(2,1)}, u32[]{:S(2)}) %copy-start.1) | copy-done | bytes 4194328
  68.2 118.9 %gram_update.1 = bf16[16,256,512]{2,1,0:T(8,128)(2,1)S(1)} custom-call(bf16[16,256,512]{2,1,0:T(8,128)(2,1)S(1)} %copy-done.1, bf16[16,256,512]{2,1,0:T(8,128)(2,1)S(1)} %copy-done), custom_call_target="tpu_custom_call" | custom-call | tf_op jit(solution)/shard_map/gram_update/pallas_call | solution.py:445
  187.2 2.0 %copy.9 = bf16[16,256,512]{2,1,0:T(8,128)(2,1)} copy(bf16[16,256,512]{2,1,0:T(8,128)(2,1)S(1)} %gram_update.1) | data formatting | bytes 8388608
Async XLA Ops:
  39.2 1.0 copy-start.2
  63.9 2.2 %copy-start = (bf16[16,256,512]{2,1,0:T(8,128)(2,1)S(1)}, bf16[16,256,512]{2,1,0:T(8,128)(2,1)}, u32[]{:S(2)}) copy-start(bf16[16,256,512]{2,1,0:T(8,128)(2,1)} %weights.1) | copy-start | bytes 12582916
  66.0 2.2 %copy-start.1 = (bf16[16,256,512]{2,1,0:T(8,128)(2,1)S(1)}, bf16[16,256,512]{2,1,0:T(8,128)(2,1)}, u32[]{:S(2)}) copy-start(bf16[16,256,512]{2,1,0:T(8,128)(2,1)} %get-tuple-element.5.mom) | copy-start | bytes 12582916

commit v4 on v3

--- a/solution.py
+++ b/solution.py
@@ -22,7 +22,7 @@
 coef_third = 2.0315
 epsilon = 1e-07
 TILE = 128
-GRANT = 34 << 20
+SPARE = 21 << 20
 MESH = pl.DeviceIdType.MESH
 F32 = jnp.float32
 BF16 = jnp.bfloat16
@@ -74,10 +74,9 @@
 
 
 class SumScatter:
-    def __init__(self, plan, per, x, near, far, sums, sems):
-        self.plan, self.per, self.x, self.near, self.far, self.sums = plan, per, x, near, far, sums
+    def __init__(self, plan, per, x, near, far, sems):
+        self.plan, self.per, self.x, self.near, self.far = plan, per, x, near, far
         self.s1, self.r1, self.s2, self.r2 = sems
-        self.second = {}
 
     @staticmethod
     def scratch(owners, per, tile):
@@ -86,7 +85,6 @@
         return [
             pltpu.VMEM((inner - 1, outer, per) + tile, BF16),
             pltpu.VMEM((outer - 1, per) + tile, BF16),
-            pltpu.VMEM((outer, per) + tile, BF16),
             dma((inner - 1, outer, per)),
             dma((inner - 1, outer, per)),
             dma((outer - 1, per)),
@@ -112,9 +110,12 @@
             for e in range(1, self.plan.inner):
                 self.first_copy(p, d, e).start()
 
+    def column(self, p, d):
+        return self.plan.row(self.plan.o_at(d), self.plan.i) * self.per + p
+
     def partial(self, p, d):
         plan = self.plan
-        total = self.x[plan.row(plan.o_at(d), plan.i) * self.per + p].astype(F32)
+        total = self.x[self.column(p, d)].astype(F32)
         for e in range(1, plan.inner):
             self.first_copy(p, d, e).wait_recv()
             total = total + self.near[e - 1, d, p].astype(F32)
@@ -123,7 +124,7 @@
     def second_copy(self, p, d):
         plan = self.plan
         return remote(
-            self.sums.at[d, p],
+            self.x.at[self.column(p, d)],
             self.far.at[d - 1, p],
             self.s2.at[d - 1, p],
             self.r2.at[d - 1, p],
@@ -131,7 +132,7 @@
         )
 
     def forward_one(self, p, d):
-        self.sums[d, p] = self.partial(p, d).astype(BF16)
+        self.x[self.column(p, d)] = self.partial(p, d).astype(BF16)
         if d:
             self.second_copy(p, d).start()
 
@@ -141,7 +142,7 @@
                 self.forward_one(p, d)
 
     def total(self, p):
-        value = self.sums[0, p].astype(F32)
+        value = self.x[self.column(p, 0)].astype(F32)
         for d in range(1, self.plan.outer):
             self.second_copy(p, d).wait_recv()
             value = value + self.far[d - 1, p].astype(F32)
@@ -221,43 +222,8 @@
                     self.second_copy(p, d, e).wait_send()
 
 
-def sum_kernel(owners, per, x, out, *scratch):
-    plan = Plan(owners)
-    plan.barrier()
-    scatter = SumScatter(plan, per, x, *scratch[:3], scratch[3:7])
-    gather = Gather(plan, per, out, scratch[7:])
-    scatter.start()
-    for p in range(per):
-        scatter.forward(p)
-    for p in range(per):
-        out[gather.mine(p)] = scatter.total(p).astype(BF16)
-        gather.start(p)
-    for p in range(per):
-        gather.forward(p)
-    for p in range(per):
-        for d in range(plan.outer):
-            gather.arrive(p, d)
-    scatter.finish()
-    gather.finish()
-
-
 def vmem():
     return pl.BlockSpec(memory_space=pltpu.VMEM)
-
-
-def all_sum(x, owners, collective_id):
-    per = x.shape[0] // owners
-    return pl.pallas_call(
-        functools.partial(sum_kernel, owners, per),
-        out_shape=jax.ShapeDtypeStruct(x.shape, x.dtype),
-        in_specs=[vmem()],
-        out_specs=vmem(),
-        scratch_shapes=SumScatter.scratch(owners, per, x.shape[1:]) + Gather.scratch(owners, per),
-        compiler_params=pltpu.CompilerParams(
-            collective_id=collective_id, has_side_effects=True, vmem_limit_bytes=20 << 20
-        ),
-        name="proj_sum",
-    )(x)
 
 
 def triangle():
@@ -380,34 +346,72 @@
         out[s, at : at + piece.shape[0]] = piece
 
 
-def store_weights(weights, mom, packed, s, out):
+def store_weights(mom, packed, s, out):
     scale_step = step_rate * 0.2 * math.sqrt(max(D, FF))
     full = unpack(packed[s], mom.shape[2], BF16)
     ortho = jnp.dot(mom[s], full, preferred_element_type=F32)
-    kept = weights[s].astype(F32) * (1.0 - step_rate * decay_rate)
+    kept = out[s].astype(F32) * (1.0 - step_rate * decay_rate)
     out[s] = (kept - scale_step * ortho).astype(BF16)
 
 
-def gram_kernel(owners, per, mom, weights, out, x, packed, *scratch):
+def store_projection(basis, grads, s, out):
+    out[s] = jnp.dot(basis[s].astype(BF16), grads[s], preferred_element_type=F32).astype(BF16)
+
+
+def store_momentum(flags, old, grads, basis, proj, s, mom):
+    low = lax.dot_general(
+        basis[s].astype(BF16), proj[s], (((0,), (0,)), ((), ())), preferred_element_type=F32
+    )
+    flag = residual_weight * flags[s].astype(F32)
+    grad_full = grads[s].astype(F32)
+    mom[s] = (momentum_decay * old[s].astype(F32) + low + flag * (grad_full - low)).astype(BF16)
+
+
+def step_kernel(owners, per, flags, old, grads, basis, weights, mom, out, fetched, px, proj, x, packed, *scratch):
     width = mom.shape[2]
+    fetch = pltpu.make_async_copy(weights, out, fetched)
+    fetch.start()
     plan = Plan(owners)
     plan.barrier()
-    scatter = SumScatter(plan, per, x, *scratch[:3], scratch[3:7])
-    gather = Gather(plan, per, packed, scratch[7:])
+    proj_scatter = SumScatter(plan, per, px, *scratch[:2], scratch[2:6])
+    proj_gather = Gather(plan, per, proj, scratch[6:10])
+    scatter = SumScatter(plan, per, x, *scratch[10:12], scratch[12:16])
+    gather = Gather(plan, per, packed, scratch[16:])
     outer, inner = plan.outer, plan.inner
+
+    def project(p):
+        @pl.loop(1, outer + 1)
+        def _(later):
+            d = lax.rem(later, outer)
+            for e in range(1, inner):
+                store_projection(basis, grads, plan.row(plan.o_at(d), plan.i_at(e)) * per + p, px)
+                proj_scatter.first_copy(p, d, e).start()
+
+    def project_own(p):
+        @pl.loop(0, outer)
+        def _(d):
+            store_projection(basis, grads, plan.row(plan.o_at(d), plan.i) * per + p, px)
+
+    def own_sum(p):
+        proj[proj_gather.mine(p)] = proj_scatter.total(p).astype(BF16)
+        proj_gather.start(p)
+
+    def prepare(s):
+        store_momentum(flags, old, grads, basis, proj, s, mom)
+        store_gram(mom, s, x)
 
     def first(p):
         @pl.loop(1, outer + 1)
         def _(later):
             d = lax.rem(later, outer)
             for e in range(1, inner):
-                store_gram(mom, plan.row(plan.o_at(d), plan.i_at(e)) * per + p, x)
+                prepare(plan.row(plan.o_at(d), plan.i_at(e)) * per + p)
                 scatter.first_copy(p, d, e).start()
 
     def own(p):
         @pl.loop(0, outer)
         def _(d):
-            store_gram(mom, plan.row(plan.o_at(d), plan.i) * per + p, x)
+            prepare(plan.row(plan.o_at(d), plan.i) * per + p)
 
     def owner_work(p):
         store_factors(scatter.total(p), width, gather.mine(p), packed)
@@ -415,12 +419,25 @@
 
     def last(p):
         for d in range(outer):
-            store_weights(weights, mom, packed, plan.row(plan.o_at(outer - d), plan.i) * per + p, out)
+            store_weights(mom, packed, plan.row(plan.o_at(outer - d), plan.i) * per + p, out)
             for s in gather.arrive(p, d):
-                store_weights(weights, mom, packed, s, out)
-
-    for p in range(per):
+                store_weights(mom, packed, s, out)
+
+    for p in range(per):
+        project(p)
+    for p in range(per):
+        project_own(p)
+    for p in range(per):
+        proj_scatter.forward(p)
+        if p:
+            own_sum(p - 1)
+    own_sum(per - 1)
+    for p in range(per):
+        proj_gather.forward(p)
+        for d in range(outer):
+            proj_gather.arrive(p, d)
         first(p)
+    for p in range(per):
         own(p)
     scatter.forward(0)
     for p in range(per):
@@ -432,94 +449,122 @@
                 scatter.forward_one(p + 1, d)
             gather.forward(p)
     gather.forward(per - 1)
+    fetch.wait()
     for p in range(per):
         last(p)
+    proj_scatter.finish()
+    proj_gather.finish()
     scatter.finish()
     gather.finish()
 
 
-def gram_update(mom, weights, owners, collective_id):
-    count, rows, width = mom.shape
+def step(refresh, old, grads, basis_t, weights, owners):
+    count, rows, width = grads.shape
     per = count // owners
     tile = (packed_rows(width), TILE)
+    line = (basis_t.shape[1], width)
+    scratch = (
+        [pltpu.SemaphoreType.DMA]
+        + [pltpu.VMEM((count,) + line, BF16)] * 2
+        + [pltpu.VMEM((count,) + tile, BF16)] * 2
+        + SumScatter.scratch(owners, per, line)
+        + Gather.scratch(owners, per)
+        + SumScatter.scratch(owners, per, tile)
+        + Gather.scratch(owners, per)
+    )
+    held = sum(2 * math.prod(one.shape) for one in scratch if one.dtype == BF16)
     return pl.pallas_call(
-        functools.partial(gram_kernel, owners, per),
-        out_shape=jax.ShapeDtypeStruct(weights.shape, weights.dtype),
-        in_specs=[vmem(), vmem()],
-        out_specs=vmem(),
-        scratch_shapes=[pltpu.VMEM((count,) + tile, BF16), pltpu.VMEM((count,) + tile, BF16)]
-        + SumScatter.scratch(owners, per, tile)
-        + Gather.scratch(owners, per),
+        functools.partial(step_kernel, owners, per),
+        out_shape=(
+            jax.ShapeDtypeStruct(weights.shape, BF16),
+            jax.ShapeDtypeStruct(weights.shape, weights.dtype),
+        ),
+        in_specs=[pl.BlockSpec(memory_space=pltpu.SMEM)]
+        + [vmem()] * 3
+        + [pl.BlockSpec(memory_space=pltpu.HBM)],
+        out_specs=(vmem(), vmem()),
+        scratch_shapes=scratch,
         compiler_params=pltpu.CompilerParams(
-            collective_id=collective_id, has_side_effects=True, vmem_limit_bytes=GRANT
+            collective_id=0, has_side_effects=True, vmem_limit_bytes=held + SPARE
         ),
-        name="gram_update",
-    )(mom, weights)
-
-
-def momentum_kernel(count, chosen, flags, bank, grad, basis, proj, new_bank, mom):
-    step = pl.program_id(0)
-
-    @pl.when(step < count)
-    def _():
-        low = lax.dot_general(
-            basis[0].astype(BF16), proj[0], (((0,), (0,)), ((), ())), preferred_element_type=F32
-        )
-        flag = residual_weight * flags[jnp.minimum(step, count - 1)].astype(F32)
-        fresh = (
-            momentum_decay * bank[0].astype(F32) + low + flag * (grad[0].astype(F32) - low)
-        ).astype(BF16)
-        new_bank[0] = fresh
-        mom[0] = fresh
-
-    @pl.when(step >= count)
-    def _():
-        new_bank[0] = bank[0]
-
-
-def momentum(order, refresh, bank, grads, basis_t, proj):
-    count, rows, width = grads.shape
-    rank = basis_t.shape[1]
-
-    def by_expert(step, chosen, flags):
-        return (chosen[step], 0, 0)
-
-    def by_sample(step, chosen, flags):
-        return (jnp.minimum(step, count - 1), 0, 0)
-
+        name="step",
+    )(refresh, old, grads, basis_t, weights)
+
+
+def take_kernel(count, order, bank, new_bank, old, stage, came, went):
+    total = bank.shape[0]
+
+    def reading(j):
+        target = old.at[j] if j < count else stage.at[j - count]
+        return pltpu.make_async_copy(bank.at[order[j]], target, came.at[j])
+
+    def writing(j):
+        return pltpu.make_async_copy(stage.at[j - count], new_bank.at[order[j]], went.at[j - count])
+
+    for j in list(range(count, total)) + list(range(count)):
+        reading(j).start()
+    for j in range(count, total):
+        reading(j).wait()
+        writing(j).start()
+    for j in range(count):
+        reading(j).wait()
+    for j in range(count, total):
+        writing(j).wait()
+
+
+def take(order, bank, count):
+    others = max(bank.shape[0] - count, 1)
+    shape = bank.shape[1:]
     return pl.pallas_call(
-        functools.partial(momentum_kernel, count),
+        functools.partial(take_kernel, count),
         out_shape=(
             jax.ShapeDtypeStruct(bank.shape, bank.dtype),
-            jax.ShapeDtypeStruct(grads.shape, BF16),
+            jax.ShapeDtypeStruct((count,) + shape, bank.dtype),
         ),
-        grid_spec=pltpu.PrefetchScalarGridSpec(
-            num_scalar_prefetch=2,
-            grid=(bank.shape[0],),
-            in_specs=[
-                pl.BlockSpec((1, rows, width), by_expert),
-                pl.BlockSpec((1, rows, width), by_sample),
-                pl.BlockSpec((1, rank, rows), by_sample),
-                pl.BlockSpec((1, rank, width), by_sample),
-            ],
-            out_specs=[
-                pl.BlockSpec((1, rows, width), by_expert),
-                pl.BlockSpec((1, rows, width), by_sample),
-            ],
-        ),
-        compiler_params=pltpu.CompilerParams(dimension_semantics=("arbitrary",)),
-        name="momentum",
-    )(order, refresh, bank, grads, basis_t, proj)
+        in_specs=[pl.BlockSpec(memory_space=pltpu.SMEM), pl.BlockSpec(memory_space=pltpu.HBM)],
+        out_specs=(pl.BlockSpec(memory_space=pltpu.HBM), vmem()),
+        scratch_shapes=[
+            pltpu.VMEM((others,) + shape, bank.dtype),
+            pltpu.SemaphoreType.DMA((bank.shape[0],)),
+            pltpu.SemaphoreType.DMA((others,)),
+        ],
+        compiler_params=pltpu.CompilerParams(vmem_limit_bytes=46 << 20),
+        name="take",
+    )(order, bank)
+
+
+def put_kernel(order, kept, mom, new_bank, sems):
+    def writing(j):
+        return pltpu.make_async_copy(mom.at[j], new_bank.at[order[j]], sems.at[j])
+
+    for j in range(mom.shape[0]):
+        writing(j).start()
+    for j in range(mom.shape[0]):
+        writing(j).wait()
+
+
+def put(order, kept, mom):
+    return pl.pallas_call(
+        put_kernel,
+        out_shape=jax.ShapeDtypeStruct(kept.shape, kept.dtype),
+        in_specs=[
+            pl.BlockSpec(memory_space=pltpu.SMEM),
+            pl.BlockSpec(memory_space=pltpu.HBM),
+            vmem(),
+        ],
+        out_specs=pl.BlockSpec(memory_space=pltpu.HBM),
+        scratch_shapes=[pltpu.SemaphoreType.DMA((mom.shape[0],))],
+        input_output_aliases={1: 0},
+        compiler_params=pltpu.CompilerParams(vmem_limit_bytes=1 << 20),
+        name="put",
+    )(order, kept, mom)
 
 
 def shards(owners, sampled, refresh, momentum_bank, weights, grads, basis):
-    basis_t = jnp.swapaxes(basis, 1, 2)
-    partial_sum = jnp.einsum(
-        "skr,srf->skf", basis_t.astype(BF16), grads, preferred_element_type=F32
-    )
-    proj = all_sum(partial_sum.astype(BF16), owners, 0)
-    new_bank, mom = momentum(sampled[0], refresh, momentum_bank, grads, basis_t, proj)
-    return new_bank, gram_update(mom, weights, owners, 1)
+    order = sampled[0]
+    kept, old = take(order, momentum_bank, weights.shape[0])
+    mom, new_weights = step(refresh, old, grads, jnp.swapaxes(basis, 1, 2), weights, owners)
+    return put(order, kept, mom), new_weights
 
 
 def solution(mesh):

time: 191 us -> 182 us (0.953)
  local copies, waits for them, and re-layouts: 7.35 us -> 3 us
  matrix products: 3.35 us -> 0 us
    unnamed x7 -> x9, local copies, waits for them, and re-layouts: 7.35 us -> 3 us
    dot_general x1 -> x0, matrix products: 3.35 us -> none  [shards(): jnp.einsum('skr,srf->skf', basis_t.astype(BF16), grads, preferred_element...]
where the time goes in v4:
time: 182 us; the launch traced here: 181 us
  Pallas kernels  178 us (98%)
  local copies, waits for them, and re-layouts  3 us (2%)
    pallas_call x1, Pallas kernels, step(): pl.pallas_call(functools.partial(step_kernel, owners, per), out_shape=(ja...  169 us
    pallas_call x1, Pallas kernels, take(): pl.pallas_call(functools.partial(take_kernel, count), out_shape=(jax.Shap...  6.11 us

profile of v4, /device:TPU:24, one launch (start us, length us, event | category | flops | bytes accessed | tf_op | source)
XLA Modules:
  0.0 181.2 jit_solution(18408434799222616030)
XLA Ops:
  0.6 0.0 copy-start.2
  0.6 0.6 copy-done.2
  1.3 0.0 copy-start
  1.3 0.0 copy-start.1
  1.3 0.0 copy-start.3
  1.3 6.1 %take.1 = (bf16[32,256,512]{2,1,0:T(8,128)(2,1)}, bf16[16,256,512]{2,1,0:T(8,128)(2,1)S(1)}) custom-call(s32[32]{0:T(128)S(1)} %bitcast.3, bf16[32,256,512]{2,1,0:T(8,128)(2,1)} %bank.1), custom_call_target="tpu_custom_call" | custom-call | tf_op jit(solution)/shard_map/take/pallas_call | solution.py:518
  7.4 0.0 copy-done
  7.4 0.3 copy-done.1
  7.7 0.0 copy-done.3
  7.7 168.7 %step.1 = (bf16[16,256,512]{2,1,0:T(8,128)(2,1)S(1)}, bf16[16,256,512]{2,1,0:T(8,128)(2,1)S(1)}) custom-call(s32[16]{0:T(128)S(1)} %copy-done.3, bf16[16,256,512]{2,1,0:T(8,128)(2,1)S(1)} %get-tuple-element.7.old, bf16[16,256,512]{2,1,0:T(8,128)(2,1)S(1)} %copy-done, f32[16,64,256]{2,1,0:T(8,128)S(1)} %bitcast.2, bf16[16,256,512]{2,1,0:T(8,128)(2,1)} %weights.1), custom_call_target="tpu_custom_call" | custom-call | tf_op jit(solution)/shard_map/step/pallas_call | solution.py:476
  176.5 2.7 %put.1 = bf16[32,256,512]{2,1,0:T(8,128)(2,1)} custom-call(s32[32]{0:T(128)S(1)} %bitcast.4, bf16[32,256,512]{2,1,0:T(8,128)(2,1)} %get-tuple-element.6.kept, bf16[16,256,512]{2,1,0:T(8,128)(2,1)S(1)} %get-tuple-element.8.mom), custom_call_target="tpu_custom_call", output_to_operand_aliasing={{}: (1, {})} | custom-call | tf_op jit(solution)/shard_map/put/pallas_call | solution.py:547
  179.2 2.0 %copy.11 = bf16[16,256,512]{2,1,0:T(8,128)(2,1)} copy(bf16[16,256,512]{2,1,0:T(8,128)(2,1)S(1)} %get-tuple-element.13) | data formatting | bytes 8388608
Async XLA Ops:
  0.6 0.7 copy-start.2
  1.3 6.2 %copy-start = (bf16[16,256,512]{2,1,0:T(8,128)(2,1)S(1)}, bf16[16,256,512]{2,1,0:T(8,128)(2,1)}, u32[]{:S(2)}) copy-start(bf16[16,256,512]{2,1,0:T(8,128)(2,1)} %grads.1) | copy-start | bytes 12582916
  1.3 6.5 %copy-start.1 = (f32[16,256,64]{1,2,0:T(8,128)S(1)}, f32[16,256,64]{1,2,0:T(8,128)}, u32[]{:S(2)}) copy-start(f32[16,256,64]{1,2,0:T(8,128)} %param.11) | copy-start | bytes 3145732
  1.3 6.5 %copy-start.3 = (s32[16]{0:T(128)S(1)}, s32[16]{0:T(128)}, u32[]{:S(2)}) copy-start(s32[16]{0:T(128)} %flags.1) | copy-start | bytes 196

commit v5 on v4

--- a/solution.py
+++ b/solution.py
@@ -434,12 +434,17 @@
     own_sum(per - 1)
     for p in range(per):
         proj_gather.forward(p)
+    for p in range(per):
         for d in range(outer):
             proj_gather.arrive(p, d)
         first(p)
-    for p in range(per):
+        if p == 0:
+            own(0)
+            scatter.forward_one(0, 1)
+    for d in list(range(2, outer)) + [0]:
+        scatter.forward_one(0, d)
+    for p in range(1, per):
         own(p)
-    scatter.forward(0)
     for p in range(per):
         if p + 1 < per:
             scatter.forward_one(p + 1, 1)

time: 182 us -> 166 us (0.912)
  Pallas kernels: 178 us -> 162 us
    pallas_call x1, Pallas kernels: 169 us -> 153 us  [step(): pl.pallas_call(functools.partial(step_kernel, owners, per), out_shape=(ja...]
where the time goes in v5:
time: 166 us; the launch traced here: 165 us
  Pallas kernels  162 us (98%)
  local copies, waits for them, and re-layouts  3 us (2%)
    pallas_call x1, Pallas kernels, step(): pl.pallas_call(functools.partial(step_kernel, owners, per), out_shape=(ja...  153 us
    pallas_call x1, Pallas kernels, take(): pl.pallas_call(functools.partial(take_kernel, count), out_shape=(jax.Shap...  6.11 us

profile of v5, /device:TPU:24, one launch (start us, length us, event | category | flops | bytes accessed | tf_op | source)
XLA Modules:
  0.0 165.3 jit_solution(83553996409381604)
XLA Ops:
  0.6 0.0 copy-start.2
  0.6 0.6 copy-done.2
  1.3 0.0 copy-start
  1.3 0.0 copy-start.1
  1.3 0.0 copy-start.3
  1.3 6.1 %take.1 = (bf16[32,256,512]{2,1,0:T(8,128)(2,1)}, bf16[16,256,512]{2,1,0:T(8,128)(2,1)S(1)}) custom-call(s32[32]{0:T(128)S(1)} %bitcast.3, bf16[32,256,512]{2,1,0:T(8,128)(2,1)} %bank.1), custom_call_target="tpu_custom_call" | custom-call | tf_op jit(solution)/shard_map/take/pallas_call | solution.py:523
  7.4 0.0 copy-done
  7.4 0.3 copy-done.1
  7.7 0.0 copy-done.3
  7.7 152.9 %step.1 = (bf16[16,256,512]{2,1,0:T(8,128)(2,1)S(1)}, bf16[16,256,512]{2,1,0:T(8,128)(2,1)S(1)}) custom-call(s32[16]{0:T(128)S(1)} %copy-done.3, bf16[16,256,512]{2,1,0:T(8,128)(2,1)S(1)} %get-tuple-element.7.old, bf16[16,256,512]{2,1,0:T(8,128)(2,1)S(1)} %copy-done, f32[16,64,256]{2,1,0:T(8,128)S(1)} %bitcast.2, bf16[16,256,512]{2,1,0:T(8,128)(2,1)} %weights.1), custom_call_target="tpu_custom_call" | custom-call | tf_op jit(solution)/shard_map/step/pallas_call | solution.py:481
  160.6 2.7 %put.1 = bf16[32,256,512]{2,1,0:T(8,128)(2,1)} custom-call(s32[32]{0:T(128)S(1)} %bitcast.4, bf16[32,256,512]{2,1,0:T(8,128)(2,1)} %get-tuple-element.6.kept, bf16[16,256,512]{2,1,0:T(8,128)(2,1)S(1)} %get-tuple-element.8.mom), custom_call_target="tpu_custom_call", output_to_operand_aliasing={{}: (1, {})} | custom-call | tf_op jit(solution)/shard_map/put/pallas_call | solution.py:552
  163.3 2.0 %copy.11 = bf16[16,256,512]{2,1,0:T(8,128)(2,1)} copy(bf16[16,256,512]{2,1,0:T(8,128)(2,1)S(1)} %get-tuple-element.13) | data formatting | bytes 8388608
Async XLA Ops:
  0.6 0.7 copy-start.2
  1.3 6.2 %copy-start = (bf16[16,256,512]{2,1,0:T(8,128)(2,1)S(1)}, bf16[16,256,512]{2,1,0:T(8,128)(2,1)}, u32[]{:S(2)}) copy-start(bf16[16,256,512]{2,1,0:T(8,128)(2,1)} %grads.1) | copy-start | bytes 12582916
  1.3 6.5 %copy-start.1 = (f32[16,256,64]{1,2,0:T(8,128)S(1)}, f32[16,256,64]{1,2,0:T(8,128)}, u32[]{:S(2)}) copy-start(f32[16,256,64]{1,2,0:T(8,128)} %param.11) | copy-start | bytes 3145732
  1.3 6.5 %copy-start.3 = (s32[16]{0:T(128)S(1)}, s32[16]{0:T(128)}, u32[]{:S(2)}) copy-start(s32[16]{0:T(128)} %flags.1) | copy-start | bytes 196
